TPU v7x, 32 devices: a whole 2x2x4 slice. The times are simulated.
32 devices in a mesh: ctx: 8 (over z, x), heads: 4 (over y, core).
Axes of the slice: x: 2, y: 2, z: 4, core: 2. Of those that a mesh axis runs over, the one named last changes fastest.
Arguments:
- activations: bfloat16 [2048, 8192], P('ctx', 'heads'), may hold values from -20 to 20
- w_query: bfloat16 [8192, 4096], P(None, 'heads'), may hold values from -0.0625 to 0.0625
- w_key: bfloat16 [8192, 1024], P(None, 'heads'), may hold values from -0.0625 to 0.0625
- w_value: bfloat16 [8192, 1024], P(None, 'heads'), may hold values from -0.0625 to 0.0625
- doc_lengths: int32 [8], replicated, may hold values from 1 to 1024, 2048 in all
- block_dest: int32 [32], replicated, may hold values from 0 to 7, as said below
- out_grad: bfloat16 [2048, 4096], P('ctx', 'heads'), may hold values from -6 to 6
Outputs:
- attention: bfloat16 [2048, 4096], P('ctx', 'heads')
- input_grad: bfloat16 [2048, 8192], P('ctx', 'heads')
Inputs may be any that keep to these rules, and one draw needn't show every extreme that they name: `block_dest`: loader block b lies on loader shard b // 4. Each loader shard sends its blocks to different context shards, and each context shard receives exactly 4 blocks, from different loader shards.
All inputs are finite; a program needn't handle non-finite values.
Results may differ from a plain program's by a relative error of at most 0.025.
The roundings to bfloat16 on the way count: a program that leaves them out, or rounds other values in their place, can miss the bound.
Values may be sent and summed in bfloat16 or wider, within the bound.
A program may use at most 128 MiB of HBM per device.

v0:
```python
import math
import jax
import jax.numpy as jnp
from jax import lax
from jax.sharding import PartitionSpec as P

HD = 128
QPK = 4
NEG = -1e30


def from_behind(value, axis, steps):
    count = lax.axis_size(axis)
    pairs = [(source, (source + steps) % count) for source in range(count)]
    return lax.ppermute(value, axis, pairs)


def layout(block_dest, block_rows):
    nblk = block_dest.shape[0]
    index = jnp.arange(nblk, dtype=jnp.int32)
    order_key = block_dest * nblk + index
    ranks = jnp.sum((order_key[None, :] < order_key[:, None]).astype(jnp.int32), axis=1)
    ctx_blocks = jnp.sum(jnp.where(ranks[None, :] == index[:, None], index[None, :], 0), axis=1)
    ctx_pos = (
        ctx_blocks[:, None] * block_rows + jnp.arange(block_rows, dtype=jnp.int32)[None, :]
    ).reshape(-1)
    return (ctx_blocks, ctx_pos)


def doc_ids(positions, doc_lengths):
    ends = jnp.cumsum(doc_lengths)
    return jnp.sum((ends[None, :] <= positions[:, None]).astype(jnp.int32), axis=1)


def spread(table, array, block_rows):
    width = array.shape[-1]
    grouped = array.reshape(table.shape[1], block_rows, width)
    moved = jnp.einsum("ab,brf->arf", table, grouped, preferred_element_type=jnp.float32)
    return moved.astype(jnp.bfloat16)


def transposed_dot(left, weight):
    return lax.dot_general(
        left, weight, (((1,), (1,)), ((), ())), preferred_element_type=jnp.float32
    )


def per_device(activations, w_query, w_key, w_value, doc_lengths, block_dest, out_grad):
    ctx_count = lax.axis_size("ctx")
    ctx_rank = lax.axis_index("ctx")
    tok_dev = activations.shape[0]
    block_rows = tok_dev * ctx_count // block_dest.shape[0]
    blocks_here = tok_dev // block_rows
    head_dim = HD
    groups = w_key.shape[1] // head_dim
    per_group = QPK
    scale = 1.0 / math.sqrt(head_dim)
    ctx_blocks, ctx_pos = layout(block_dest, block_rows)
    ctx_doc = doc_ids(ctx_pos, doc_lengths)
    my_pos = lax.dynamic_slice_in_dim(ctx_pos, ctx_rank * tok_dev, tok_dev, 0)
    my_doc = lax.dynamic_slice_in_dim(ctx_doc, ctx_rank * tok_dev, tok_dev, 0)
    piece = lax.all_gather(activations, "heads", axis=1, tiled=True)
    rows = piece.shape[1]
    proj_q = jnp.dot(piece, w_query, preferred_element_type=jnp.float32)
    proj_k = jnp.dot(piece, w_key, preferred_element_type=jnp.float32)
    proj_v = jnp.dot(piece, w_value, preferred_element_type=jnp.float32)
    loader_q = proj_q.astype(jnp.bfloat16)
    loader_k = proj_k.astype(jnp.bfloat16)
    loader_v = proj_v.astype(jnp.bfloat16)
    slots = jnp.arange(ctx_count, dtype=jnp.int32)
    my_dest = lax.dynamic_slice_in_dim(block_dest, ctx_rank * blocks_here, blocks_here, 0)
    send_map = (my_dest[None, :] == slots[:, None]).astype(jnp.bfloat16)
    mine = lax.dynamic_slice_in_dim(ctx_blocks, ctx_rank * blocks_here, blocks_here, 0)
    source = mine // blocks_here
    take_map = (source[:, None] == slots[None, :]).astype(jnp.bfloat16)
    recv_q, recv_k, recv_v = (
        lax.all_to_all(
            spread(send_map, loader_q, block_rows), "ctx", split_axis=0, concat_axis=0, tiled=True
        ),
        lax.all_to_all(
            spread(send_map, loader_k, block_rows), "ctx", split_axis=0, concat_axis=0, tiled=True
        ),
        lax.all_to_all(
            spread(send_map, loader_v, block_rows), "ctx", split_axis=0, concat_axis=0, tiled=True
        ),
    )
    ctx_q = spread(take_map, recv_q.reshape(ctx_count * block_rows, -1), block_rows).reshape(
        tok_dev, -1
    )
    ctx_k = spread(take_map, recv_k.reshape(ctx_count * block_rows, -1), block_rows).reshape(
        tok_dev, -1
    )
    ctx_v = spread(take_map, recv_v.reshape(ctx_count * block_rows, -1), block_rows).reshape(
        tok_dev, -1
    )
    query_four = ctx_q.reshape(tok_dev, groups, per_group, head_dim)

    def visible(key_pos, key_doc):
        return (my_doc[:, None] == key_doc[None, :]) & (key_pos[None, :] <= my_pos[:, None])

    def attend(state, key_blk, value_blk, key_pos, key_doc):
        mask = visible(key_pos, key_doc)

        def attend_run(inner):
            m_old, l_old, accum = inner
            scores = (
                jnp.einsum(
                    "tgqe,sge->gqts", query_four, key_blk, preferred_element_type=jnp.float32
                )
                * scale
            )
            scores = jnp.where(mask[None, None], scores, NEG)
            m_new = jnp.maximum(m_old, jnp.max(scores, axis=-1))
            factor = jnp.exp(m_old - m_new)
            probs = jnp.where(mask[None, None], jnp.exp(scores - m_new[..., None]), 0.0)
            l_new = l_old * factor + jnp.sum(probs, axis=-1)
            accum = accum * factor[..., None] + jnp.einsum(
                "gqts,sge->gqte",
                probs,
                value_blk.astype(jnp.float32),
                precision=lax.Precision.HIGHEST,
                preferred_element_type=jnp.float32,
            )
            return (m_new, l_new, accum)

        return lax.cond(jnp.any(mask), attend_run, lambda inner: inner, state)

    start_state = (
        jnp.full((groups, per_group, tok_dev), NEG, jnp.float32),
        jnp.zeros((groups, per_group, tok_dev), jnp.float32),
        jnp.zeros((groups, per_group, tok_dev, head_dim), jnp.float32),
    )
    grad_four = out_grad.reshape(tok_dev, groups, per_group, head_dim)

    def grads_over(dquery, key_piece, value_piece, start, lse, delta):
        rows = key_piece.shape[0]
        width = math.gcd(rows, 512)

        def grads_one_block(index, inner):
            dq_sum, dk_rows, dv_rows = inner
            offset = index * width
            key_blk = key_piece.reshape(width, groups, head_dim)
            value_blk = value_piece.reshape(width, groups, head_dim)
            key_pos = lax.dynamic_slice_in_dim(ctx_pos, start + offset, width, 0)
            key_doc = lax.dynamic_slice_in_dim(ctx_doc, start + offset, width, 0)
            mask = visible(key_pos, key_doc)

            def one_run(unused):
                scores = (
                    jnp.einsum(
                        "tgqe,sge->gqts", query_four, key_blk, preferred_element_type=jnp.float32
                    )
                    * scale
                )
                weights = jnp.where(mask[None, None], jnp.exp(scores - lse[..., None]), 0.0)
                weights_b = weights.astype(jnp.bfloat16)
                dv_blk = jnp.einsum(
                    "gqts,tgqe->sge", weights_b, grad_four, preferred_element_type=jnp.float32
                )
                dprob = jnp.einsum(
                    "tgqe,sge->gqts", grad_four, value_blk, preferred_element_type=jnp.float32
                )
                dscore = (weights * (dprob - delta[..., None]) * scale).astype(jnp.bfloat16)
                dq_add = jnp.einsum(
                    "gqts,sge->tgqe", dscore, key_blk, preferred_element_type=jnp.float32
                )
                dk_blk = jnp.einsum(
                    "gqts,tgqe->sge", dscore, query_four, preferred_element_type=jnp.float32
                )
                return (dq_add, dk_blk, dv_blk)

            def skip(unused):
                return (
                    jnp.zeros((tok_dev, groups, per_group, head_dim), jnp.float32),
                    jnp.zeros((width, groups, head_dim), jnp.float32),
                    jnp.zeros((width, groups, head_dim), jnp.float32),
                )

            dq_add, dk_blk, dv_blk = lax.cond(jnp.any(mask), one_run, skip, 0)
            dk_rows = dk_blk.reshape(width, groups * head_dim)
            dv_rows = dv_blk.reshape(width, groups * head_dim)
            return (dq_sum + dq_add, dk_rows, dv_rows)

        empty_rows = jnp.zeros((rows, groups * head_dim), jnp.float32)
        return lax.fori_loop(0, rows // width, grads_one_block, (dquery, empty_rows, empty_rows))

    dq_start = jnp.zeros((tok_dev, groups, per_group, head_dim), jnp.float32)
    key_piece = lax.all_gather(ctx_k, "ctx", axis=0, tiled=True)
    value_piece = lax.all_gather(ctx_v, "ctx", axis=0, tiled=True)
    rows = key_piece.shape[0]
    width = math.gcd(rows, 512)

    def fold_one_block(index, inner):
        offset = index * width
        key_blk = lax.dynamic_slice_in_dim(key_piece, offset, width, 0).reshape(
            width, groups, head_dim
        )
        value_blk = lax.dynamic_slice_in_dim(value_piece, offset, width, 0).reshape(
            width, groups, head_dim
        )
        key_pos = lax.dynamic_slice_in_dim(ctx_pos, offset, width, 0)
        key_doc = lax.dynamic_slice_in_dim(ctx_doc, offset, width, 0)
        return attend(inner, key_blk, value_blk, key_pos, key_doc)

    m_end, l_end, accum = lax.fori_loop(0, rows // width, fold_one_block, start_state)
    attn = (accum / l_end[..., None]).astype(jnp.bfloat16)
    attention = attn.transpose(2, 0, 1, 3).reshape(tok_dev, groups * per_group * head_dim)
    lse = m_end + jnp.log(l_end)
    attn_four = attention.reshape(tok_dev, groups, per_group, head_dim)
    delta = jnp.einsum(
        "tgqe,tgqe->gqt", grad_four.astype(jnp.float32), attn_four.astype(jnp.float32)
    )

    def turn(step, inner):
        dquery, key_now, value_now, dk_now, dv_now = inner
        owner = jnp.mod(ctx_rank - step, ctx_count)
        dquery, dk_add, dv_add = grads_over(dquery, key_now, value_now, owner * tok_dev, lse, delta)
        dk_now, dv_now = (
            from_behind((dk_now + dk_add).astype(jnp.bfloat16), "ctx", 1).astype(jnp.float32),
            from_behind((dv_now + dv_add).astype(jnp.bfloat16), "ctx", 1).astype(jnp.float32),
        )
        key_now, value_now = from_behind((key_now, value_now), "ctx", 1)
        return (dquery, key_now, value_now, dk_now, dv_now)

    zero_grads = jnp.zeros((tok_dev, groups * head_dim), jnp.float32)
    dquery, unused_k, unused_v, dkey, dvalue = lax.fori_loop(
        0, ctx_count, turn, (dq_start, ctx_k, ctx_v, zero_grads, zero_grads)
    )
    dq_ctx = dquery.reshape(tok_dev, groups * per_group * head_dim).astype(jnp.bfloat16)
    dk_ctx = dkey.astype(jnp.bfloat16)
    dv_ctx = dvalue.astype(jnp.bfloat16)
    back_map = take_map.T
    home_q, home_k, home_v = (
        lax.all_to_all(
            spread(back_map, dq_ctx, block_rows), "ctx", split_axis=0, concat_axis=0, tiled=True
        ),
        lax.all_to_all(
            spread(back_map, dk_ctx, block_rows), "ctx", split_axis=0, concat_axis=0, tiled=True
        ),
        lax.all_to_all(
            spread(back_map, dv_ctx, block_rows), "ctx", split_axis=0, concat_axis=0, tiled=True
        ),
    )
    pick_map = send_map.T
    dq_loader = spread(pick_map, home_q.reshape(ctx_count * block_rows, -1), block_rows).reshape(
        tok_dev, -1
    )
    dk_loader = spread(pick_map, home_k.reshape(ctx_count * block_rows, -1), block_rows).reshape(
        tok_dev, -1
    )
    dv_loader = spread(pick_map, home_v.reshape(ctx_count * block_rows, -1), block_rows).reshape(
        tok_dev, -1
    )
    grad_terms = (
        transposed_dot(dq_loader, w_query)
        + transposed_dot(dk_loader, w_key)
        + transposed_dot(dv_loader, w_value)
    )
    input_grad = lax.psum_scatter(
        grad_terms.astype(jnp.bfloat16), "heads", scatter_dimension=1, tiled=True
    )
    return (attention, input_grad)


def solution(mesh):
    return jax.shard_map(
        per_device,
        mesh=mesh,
        in_specs=(
            P("ctx", "heads"),
            P(None, "heads"),
            P(None, "heads"),
            P(None, "heads"),
            P(),
            P(),
            P("ctx", "heads"),
        ),
        out_specs=(P("ctx", "heads"), P("ctx", "heads")),
        check_vma=False,
    )
```

profile of v0, /device:TPU:0, one launch (start us, length us, event | category | flops | bytes accessed | tf_op | source)
XLA Modules:
  0.0 553.3 jit_solution(3324979120740839685)
XLA Ops:
  9.7 37.1 %all-gather.4.cloned.1.call-done = bf16[256,8192]{1,0:T(8,128)(2,1)} async-done(((bf16[256,2048]{1,0:T(8,128)(2,1)}), bf16[256,8192]{1,0:T(8,128)(2,1)}) %all-gather.4.cloned.1.call-update) | async-done | bytes 4194320 | tf_op jit(solution)/shard_map/all_gather | solution.py:62
  46.8 4.7 convolution_convert_fusion.13
  52.6 5.5 all-to-all-start.2
  58.1 4.7 convolution_convert_fusion.14
  63.9 3.5 all-to-all-done.2
  67.4 3.6 all-to-all-start
  72.1 11.5 %convolution_convert_fusion.4 = bf16[256,1024]{1,0:T(8,128)(2,1)S(1)} fusion(bf16[256,8192]{1,0:T(8,128)(2,1)} %all-gather.4.cloned.1.call-done, bf16[8192,1024]{1,0:T(8,128)(2,1)} %param.16), kind=kOutput, calls=%fused_computation.45 | convolution fusion | flops 4295229440 | bytes 21495808 | tf_op jit(solution)/shard_map/dot_general | solution.py:64
  85.8 6.0 %all-to-all-start.1 = ((bf16[8,64,1024]{2,1,0:T(8,128)(2,1)}), bf16[8,64,1024]{2,1,0:T(8,128)(2,1)S(1)}, u32[]{:S(2)}, u32[]{:S(2)}) async-start(bf16[8,64,1024]{2,1,0:T(8,128)(2,1)} %copy.107), calls=%async_computation.1 | async-start | bytes 2097152 | tf_op jit(solution)/shard_map/all_to_all | solution.py:77
  98.1 27.5 %all-to-all-done.1 = bf16[8,64,1024]{2,1,0:T(8,128)(2,1)S(1)} async-done(((bf16[8,64,1024]{2,1,0:T(8,128)(2,1)}), bf16[8,64,1024]{2,1,0:T(8,128)(2,1)S(1)}, u32[]{:S(2)}, u32[]{:S(2)}) %all-to-all-start.1) | async-done | bytes 1048608 | tf_op jit(solution)/shard_map/all_to_all | solution.py:77
  129.8 36.9 %all-gather.6.cloned.1.call-done = bf16[2048,256]{1,0:T(8,128)(2,1)} async-done(((bf16[256,256]{1,0:T(8,128)(2,1)}), bf16[2048,256]{1,0:T(8,128)(2,1)}) %all-gather.6.cloned.1.call-update) | async-done | bytes 1048592 | tf_op jit(solution)/shard_map/all_gather | solution.py:188
  166.6 2.3 copy.114
  170.0 47.4 %while.56 = (s32[]{:T(128)}, f32[2,4,256]{2,1,0:T(4,128)S(1)}, f32[2,4,256]{2,1,0:T(4,128)S(1)}, f32[2,4,256,128]{3,2,1,0:T(8,128)}, s32[256]{0:T(256)}, /*index...) while((s32[]{:T(128)}, f32[2,4,256]{2,1,0:T(4,128)S(1)}, ...), condition=%wide.region_10.11_spmd, body=%wide.region_4.10_spmd.sunk | while | flops 1892683776 | bytes 25835900 | solution.py:205
  173.7 8.2 %conditional.5 = ((f32[2,4,256]{2,1,0:T(4,128)S(1)}, f32[2,4,256]{2,1,0:T(4,128)S(1)}, f32[2,4,256,128]{3,2,1,0:T(8,128)})) conditional(s32[]{:T(128)} %convert_element_type.201, (f32[2,4,256]{2,1,0:T(4,128)S(1)}, f32[2,4,256]{2,1,0:T(4,128)S(1)}, f32[2,4,256,128]{3,2,1,0:T(8,128)}) %tuple.116, (pred[256,512]{0,1:T(8,128)(4,1)S(1)}, ...), branch_computations={%region_6.6_spmd, %region_7.9_spmd} | conditional | flops 1892159488 | bytes 25690204 | solution.py:126
  176.6 4.2 fusion.8
  185.5 8.2 %conditional.5 = ((f32[2,4,256]{2,1,0:T(4,128)S(1)}, f32[2,4,256]{2,1,0:T(4,128)S(1)}, f32[2,4,256,128]{3,2,1,0:T(8,128)})) conditional(s32[]{:T(128)} %convert_element_type.201, (f32[2,4,256]{2,1,0:T(4,128)S(1)}, f32[2,4,256]{2,1,0:T(4,128)S(1)}, f32[2,4,256,128]{3,2,1,0:T(8,128)}) %tuple.116, (pred[256,512]{0,1:T(8,128)(4,1)S(1)}, ...), branch_computations={%region_6.6_spmd, %region_7.9_spmd} | conditional | flops 1892159488 | bytes 25690204 | solution.py:126
  188.5 4.2 fusion.8
  197.4 8.2 %conditional.5 = ((f32[2,4,256]{2,1,0:T(4,128)S(1)}, f32[2,4,256]{2,1,0:T(4,128)S(1)}, f32[2,4,256,128]{3,2,1,0:T(8,128)})) conditional(s32[]{:T(128)} %convert_element_type.201, (f32[2,4,256]{2,1,0:T(4,128)S(1)}, f32[2,4,256]{2,1,0:T(4,128)S(1)}, f32[2,4,256,128]{3,2,1,0:T(8,128)}) %tuple.116, (pred[256,512]{0,1:T(8,128)(4,1)S(1)}, ...), branch_computations={%region_6.6_spmd, %region_7.9_spmd} | conditional | flops 1892159488 | bytes 25690204 | solution.py:126
  200.4 4.2 fusion.8
  209.2 8.2 %conditional.5 = ((f32[2,4,256]{2,1,0:T(4,128)S(1)}, f32[2,4,256]{2,1,0:T(4,128)S(1)}, f32[2,4,256,128]{3,2,1,0:T(8,128)})) conditional(s32[]{:T(128)} %convert_element_type.201, (f32[2,4,256]{2,1,0:T(4,128)S(1)}, f32[2,4,256]{2,1,0:T(4,128)S(1)}, f32[2,4,256,128]{3,2,1,0:T(8,128)}) %tuple.116, (pred[256,512]{0,1:T(8,128)(4,1)S(1)}, ...), branch_computations={%region_6.6_spmd, %region_7.9_spmd} | conditional | flops 1892159488 | bytes 25690204 | solution.py:126
  212.2 4.2 fusion.8
  217.4 2.7 fusion.51
  222.4 202.9 %while.57 = (s32[]{:T(128)}, f32[256,2,4,128]{3,0,2,1:T(8,128)S(1)}, bf16[256,256]{1,0:T(8,128)(2,1)}, bf16[256,256]{1,0:T(8,128)(2,1)}, f32[256,256]{0,1:T(8,12...) while((s32[]{:T(128)}, ...), condition=%wide.region_15.16_spmd.clone, body=%wide.region_11.15_spmd.clone.sunk | while | flops 676593664 | bytes 24142468 | solution.py:226
  229.1 2.1 fusion.83
  231.7 5.6 %conditional.6 = (f32[256,2,4,128]{3,0,2,1:T(8,128)S(1)}, f32[256,256]{0,1:T(8,128)S(1)}, f32[256,256]{0,1:T(8,128)S(1)}) conditional(s32[]{:T(128)} %convert_element_type.204, () %tuple.120, (pred[256,256]{0,1:T(8,128)(4,1)}, bf16[256,256]{1,0:T(8,128)(2,1)}, bf16[256,2,4,128]{0,3,2,1:T(8,128)(2,1)}, f32[2,4,256]{2,1,0:T(4,128)}, ...), branch_computations={%region_13.13_spmd, %region_14.14_spmd} | conditional | flops 675282944 | bytes 16203828 | solution.py:179
  240.0 5.5 collective-permute-done.3
  252.9 2.1 fusion.83
  255.6 5.6 %conditional.6 = (f32[256,2,4,128]{3,0,2,1:T(8,128)S(1)}, f32[256,256]{0,1:T(8,128)S(1)}, f32[256,256]{0,1:T(8,128)S(1)}) conditional(s32[]{:T(128)} %convert_element_type.204, () %tuple.120, (pred[256,256]{0,1:T(8,128)(4,1)}, bf16[256,256]{1,0:T(8,128)(2,1)}, bf16[256,2,4,128]{0,3,2,1:T(8,128)(2,1)}, f32[2,4,256]{2,1,0:T(4,128)}, ...), branch_computations={%region_13.13_spmd, %region_14.14_spmd} | conditional | flops 675282944 | bytes 16203828 | solution.py:179
  262.8 2.3 collective-permute-start.2
  265.4 3.6 collective-permute-done.3
  277.3 2.1 fusion.83
  279.9 5.6 %conditional.6 = (f32[256,2,4,128]{3,0,2,1:T(8,128)S(1)}, f32[256,256]{0,1:T(8,128)S(1)}, f32[256,256]{0,1:T(8,128)S(1)}) conditional(s32[]{:T(128)} %convert_element_type.204, () %tuple.120, (pred[256,256]{0,1:T(8,128)(4,1)}, bf16[256,256]{1,0:T(8,128)(2,1)}, bf16[256,2,4,128]{0,3,2,1:T(8,128)(2,1)}, f32[2,4,256]{2,1,0:T(4,128)}, ...), branch_computations={%region_13.13_spmd, %region_14.14_spmd} | conditional | flops 675282944 | bytes 16203828 | solution.py:179
  289.7 3.6 collective-permute-done.3
  293.3 2.5 collective-permute-done.2
  301.4 2.1 fusion.83
  304.1 5.6 %conditional.6 = (f32[256,2,4,128]{3,0,2,1:T(8,128)S(1)}, f32[256,256]{0,1:T(8,128)S(1)}, f32[256,256]{0,1:T(8,128)S(1)}) conditional(s32[]{:T(128)} %convert_element_type.204, () %tuple.120, (pred[256,256]{0,1:T(8,128)(4,1)}, bf16[256,256]{1,0:T(8,128)(2,1)}, bf16[256,2,4,128]{0,3,2,1:T(8,128)(2,1)}, f32[2,4,256]{2,1,0:T(4,128)}, ...), branch_computations={%region_13.13_spmd, %region_14.14_spmd} | conditional | flops 675282944 | bytes 16203828 | solution.py:179
  309.7 2.5 collective-permute-start.3
  314.4 3.0 collective-permute-done.3
  317.4 3.7 collective-permute-done.2
  325.1 2.3 collective-permute-start.1
  328.9 2.1 fusion.83
  331.5 5.6 %conditional.6 = (f32[256,2,4,128]{3,0,2,1:T(8,128)S(1)}, f32[256,256]{0,1:T(8,128)S(1)}, f32[256,256]{0,1:T(8,128)S(1)}) conditional(s32[]{:T(128)} %convert_element_type.204, () %tuple.120, (pred[256,256]{0,1:T(8,128)(4,1)}, bf16[256,256]{1,0:T(8,128)(2,1)}, bf16[256,2,4,128]{0,3,2,1:T(8,128)(2,1)}, f32[2,4,256]{2,1,0:T(4,128)}, ...), branch_computations={%region_13.13_spmd, %region_14.14_spmd} | conditional | flops 675282944 | bytes 16203828 | solution.py:179
  339.2 7.0 %collective-permute-done.3 = bf16[256,256]{0,1:T(8,128)(2,1)S(1)} collective-permute-done((bf16[256,256]{0,1:T(8,128)(2,1)S(1)}, bf16[256,256]{0,1:T(8,128)(2,1)S(1)}, u32[]{:S(2)}, u32[]{:S(2)}) %collective-permute-start.3) | collective-permute-done | bytes 131104 | tf_op jit(solution)/shard_map/while/body/eval_jaxpr/ppermute | solution.py:15
  346.3 2.7 collective-permute-done.2
  354.4 2.1 fusion.83
  357.0 5.6 %conditional.6 = (f32[256,2,4,128]{3,0,2,1:T(8,128)S(1)}, f32[256,256]{0,1:T(8,128)S(1)}, f32[256,256]{0,1:T(8,128)S(1)}) conditional(s32[]{:T(128)} %convert_element_type.204, () %tuple.120, (pred[256,256]{0,1:T(8,128)(4,1)}, bf16[256,256]{1,0:T(8,128)(2,1)}, bf16[256,2,4,128]{0,3,2,1:T(8,128)(2,1)}, f32[2,4,256]{2,1,0:T(4,128)}, ...), branch_computations={%region_13.13_spmd, %region_14.14_spmd} | conditional | flops 675282944 | bytes 16203828 | solution.py:179
  363.7 2.7 collective-permute-start.2
  366.7 4.1 collective-permute-done.3
  381.7 5.6 %conditional.6 = (f32[256,2,4,128]{3,0,2,1:T(8,128)S(1)}, f32[256,256]{0,1:T(8,128)S(1)}, f32[256,256]{0,1:T(8,128)S(1)}) conditional(s32[]{:T(128)} %convert_element_type.204, () %tuple.120, (pred[256,256]{0,1:T(8,128)(4,1)}, bf16[256,256]{1,0:T(8,128)(2,1)}, bf16[256,2,4,128]{0,3,2,1:T(8,128)(2,1)}, f32[2,4,256]{2,1,0:T(4,128)}, ...), branch_computations={%region_13.13_spmd, %region_14.14_spmd} | conditional | flops 675282944 | bytes 16203828 | solution.py:179
  389.0 2.9 collective-permute-start.2
  392.2 4.1 collective-permute-done.3
  401.7 2.3 collective-permute-start.1
  405.5 2.1 fusion.83
  408.2 5.6 %conditional.6 = (f32[256,2,4,128]{3,0,2,1:T(8,128)S(1)}, f32[256,256]{0,1:T(8,128)S(1)}, f32[256,256]{0,1:T(8,128)S(1)}) conditional(s32[]{:T(128)} %convert_element_type.204, () %tuple.120, (pred[256,256]{0,1:T(8,128)(4,1)}, bf16[256,256]{1,0:T(8,128)(2,1)}, bf16[256,2,4,128]{0,3,2,1:T(8,128)(2,1)}, f32[2,4,256]{2,1,0:T(4,128)}, ...), branch_computations={%region_13.13_spmd, %region_14.14_spmd} | conditional | flops 675282944 | bytes 16203828 | solution.py:179
  416.9 6.0 %collective-permute-done.3 = bf16[256,256]{0,1:T(8,128)(2,1)S(1)} collective-permute-done((bf16[256,256]{0,1:T(8,128)(2,1)S(1)}, bf16[256,256]{0,1:T(8,128)(2,1)S(1)}, u32[]{:S(2)}, u32[]{:S(2)}) %collective-permute-start.3) | collective-permute-done | bytes 131104 | tf_op jit(solution)/shard_map/while/body/eval_jaxpr/ppermute | solution.py:15
  426.5 3.4 all-to-all-start.5
  432.1 6.0 %all-to-all-done.5 = bf16[8,64,256]{2,1,0:T(8,128)(2,1)S(1)} async-done(((bf16[8,64,256]{2,1,0:T(8,128)(2,1)}), bf16[8,64,256]{2,1,0:T(8,128)(2,1)S(1)}, u32[]{:S(2)}, u32[]{:S(2)}) %all-to-all-start.5) | async-done | bytes 262176 | tf_op jit(solution)/shard_map/all_to_all | solution.py:240
  438.1 3.6 all-to-all-start.4
  444.8 9.6 %all-to-all-done.4 = bf16[8,64,256]{2,1,0:T(8,128)(2,1)S(1)} async-done(((bf16[8,64,256]{2,1,0:T(8,128)(2,1)}), bf16[8,64,256]{2,1,0:T(8,128)(2,1)S(1)}, u32[]{:S(2)}, u32[]{:S(2)}) %all-to-all-start.4) | async-done | bytes 262176 | tf_op jit(solution)/shard_map/all_to_all | solution.py:237
  454.5 3.6 all-to-all-start.3
  458.7 15.6 %all-to-all-done.3 = bf16[8,64,1024]{2,1,0:T(8,128)(2,1)S(1)} async-done(((bf16[8,64,1024]{2,1,0:T(8,128)(2,1)}), bf16[8,64,1024]{2,1,0:T(8,128)(2,1)S(1)}, u32[]{:S(2)}, u32[]{:S(2)}) %all-to-all-start.3) | async-done | bytes 1048608 | tf_op jit(solution)/shard_map/all_to_all | solution.py:234
  475.3 18.9 %fusion.56 = f32[256,8192]{1,0:T(8,128)} fusion(bf16[256,1024]{1,0:T(8,128)(2,1)S(1)} %bitcast.128, bf16[8192,1024]{1,0:T(8,128)(2,1)} %param.16), kind=kOutput, calls=%fused_computation.91 | convolution fusion | flops 4294967296 | bytes 25690112 | tf_op jit(solution)/shard_map/dot_general | solution.py:43
  494.2 6.1 %convolution_add_fusion.1 = f32[256,8192]{1,0:T(8,128)S(1)} fusion(f32[256,8192]{1,0:T(8,128)} %fusion.56, bf16[256,256]{1,0:T(8,128)(2,1)S(1)} %bitcast.133, bf16[8192,256]{1,0:T(8,128)(2,1)} %param.17), kind=kOutput, calls=%fused_computation.39 | convolution fusion | flops 1075838976 | bytes 21102592 | tf_op jit(solution)/shard_map/dot_general | solution.py:43
  500.3 3.3 fusion.24
  506.2 40.6 %reduce-scatter.2.cloned.1.call-done = bf16[256,2048]{1,0:T(8,128)(2,1)} async-done(((bf16[256,8192]{1,0:T(8,128)(2,1)}), bf16[256,2048]{1,0:T(8,128)(2,1)}) %reduce-scatter.2.cloned.1.call-update) | async-done | bytes 1048592 | tf_op jit(solution)/shard_map/reduce_scatter | solution.py:259
  (327 shorter events, 182.3 us)
Async XLA Ops:
  7.2 39.6 %all-gather.4.cloned.1.call-start = ((), (), s32[]{:S(2)}) async-start(), calls=%async_computation.7 | async-start | bytes 5242880 | tf_op jit(solution)/shard_map/all_gather | solution.py:62
  8.6 75.0 %copy-start.6 = (s32[4]{0:T(128)}, s32[4]{0:T(128)S(1)}, u32[]{:S(2)}) copy-start(s32[4]{0:T(128)S(1)} %dynamic_slice.75) | copy-start | bytes 52
  9.7 115.9 %copy-start.8 = (s32[4]{0:T(128)}, s32[4]{0:T(128)S(1)}, u32[]{:S(2)}) copy-start(s32[4]{0:T(128)S(1)} %and_select_fusion) | copy-start | bytes 52
  52.6 14.8 %all-to-all-start.2 = ((bf16[8,64,256]{2,1,0:T(8,128)(2,1)}), bf16[8,64,256]{2,1,0:T(8,128)(2,1)S(1)}, u32[]{:S(2)}, u32[]{:S(2)}) async-start(bf16[8,64,256]{2,1,0:T(8,128)(2,1)} %copy.111), calls=%async_computation.2 | async-start | bytes 524288 | tf_op jit(solution)/shard_map/all_to_all | solution.py:83
  67.4 18.4 %all-to-all-start = ((bf16[8,64,256]{2,1,0:T(8,128)(2,1)}), bf16[8,64,256]{2,1,0:T(8,128)(2,1)S(1)}, u32[]{:S(2)}, u32[]{:S(2)}) async-start(bf16[8,64,256]{2,1,0:T(8,128)(2,1)} %copy.103), calls=%async_computation | async-start | bytes 524288 | tf_op jit(solution)/shard_map/all_to_all | solution.py:80
  71.0 57.1 %all-gather.8.cloned.1.call-start = ((), (), s32[]{:S(2)}) async-start(), calls=%async_computation.9 | async-start | bytes 1179648 | tf_op jit(solution)/shard_map/all_gather | solution.py:189
  83.6 9.2 %copy-start.10 = (s32[8]{0:T(128)S(1)}, s32[8]{0:T(128)}, u32[]{:S(2)}) copy-start(s32[8]{0:T(128)} %param.19) | copy-start | bytes 100
  83.6 14.2 %copy-start.5 = (bf16[256,1024]{1,0:T(8,128)(2,1)S(1)}, bf16[256,1024]{1,0:T(8,128)(2,1)}, u32[]{:S(2)}) copy-start(bf16[256,1024]{1,0:T(8,128)(2,1)} %param.21) | copy-start | bytes 1572868
  85.8 39.7 %all-to-all-start.1 = ((bf16[8,64,1024]{2,1,0:T(8,128)(2,1)}), bf16[8,64,1024]{2,1,0:T(8,128)(2,1)S(1)}, u32[]{:S(2)}, u32[]{:S(2)}) async-start(bf16[8,64,1024]{2,1,0:T(8,128)(2,1)} %copy.107), calls=%async_computation.1 | async-start | bytes 2097152 | tf_op jit(solution)/shard_map/all_to_all | solution.py:77
  91.8 74.8 %all-gather.6.cloned.1.call-start = ((), (), s32[]{:S(2)}) async-start(), calls=%async_computation.8 | async-start | bytes 1179648 | tf_op jit(solution)/shard_map/all_gather | solution.py:188
  174.7 2.0 copy-start.1
  180.9 1.0 copy-start.2
  186.5 2.0 copy-start.1
  198.4 2.0 copy-start.1
  204.6 1.0 copy-start.2
  210.3 2.0 copy-start.1
  222.4 203.0 %copy-start.9 = (s32[4]{0:T(128)S(1)}, s32[4]{0:T(128)}, u32[]{:S(2)}) copy-start(s32[4]{0:T(128)} %copy-done.8) | copy-start | bytes 52
  224.0 23.6 %collective-permute-start = (bf16[256,256]{1,0:T(8,128)(2,1)}, bf16[256,256]{1,0:T(8,128)(2,1)}, u32[]{:S(2)}, u32[]{:S(2)}) collective-permute-start(bf16[256,256]{1,0:T(8,128)(2,1)} %copy.227), channel_id=1, source_target_pairs={{0,4},{4,8},{8,12},{12,16},{16,20},{20,24},{24,28},{28,0},{1,5},{5... | collective-permute-start | bytes 393224 | tf_op jit(solution)/shard_map/while/body/eval_jaxpr/ppermute | solution.py:15
  226.1 21.5 %collective-permute-start.1 = (bf16[256,256]{1,0:T(8,128)(2,1)}, bf16[256,256]{1,0:T(8,128)(2,1)}, u32[]{:S(2)}, u32[]{:S(2)}) collective-permute-start(bf16[256,256]{1,0:T(8,128)(2,1)} %copy.228), channel_id=1, source_target_pairs={{0,4},{4,8},{8,12},{12,16},{16,20},{20,24},{24,28},{28,0},{1,5},{5... | collective-permute-start | bytes 393224 | tf_op jit(solution)/shard_map/while/body/eval_jaxpr/ppermute | solution.py:15
  233.6 2.6 copy-start
  237.3 8.2 %collective-permute-start.3 = (bf16[256,256]{0,1:T(8,128)(2,1)S(1)}, bf16[256,256]{0,1:T(8,128)(2,1)S(1)}, u32[]{:S(2)}, u32[]{:S(2)}) collective-permute-start(bf16[256,256]{0,1:T(8,128)(2,1)S(1)} %fusion.85), channel_id=1, source_target_pairs={{0,4},{4,8},{8,12},{12,16},{16,20},{20,24},{24,28},{28,0},{1,5},{5... | collective-permute-start | bytes 393224 | tf_op jit(solution)/shard_map/while/body/eval_jaxpr/ppermute | solution.py:15
  238.0 8.9 %collective-permute-start.2 = (bf16[256,256]{0,1:T(8,128)(2,1)S(1)}, bf16[256,256]{0,1:T(8,128)(2,1)S(1)}, u32[]{:S(2)}, u32[]{:S(2)}) collective-permute-start(bf16[256,256]{0,1:T(8,128)(2,1)S(1)} %fusion.84), channel_id=1, source_target_pairs={{0,4},{4,8},{8,12},{12,16},{16,20},{20,24},{24,28},{28,0},{1,5},{5... | collective-permute-start | bytes 393224 | tf_op jit(solution)/shard_map/while/body/eval_jaxpr/ppermute | solution.py:15
  249.2 22.0 %collective-permute-start = (bf16[256,256]{1,0:T(8,128)(2,1)}, bf16[256,256]{1,0:T(8,128)(2,1)}, u32[]{:S(2)}, u32[]{:S(2)}) collective-permute-start(bf16[256,256]{1,0:T(8,128)(2,1)} %copy.227), channel_id=1, source_target_pairs={{0,4},{4,8},{8,12},{12,16},{16,20},{20,24},{24,28},{28,0},{1,5},{5... | collective-permute-start | bytes 393224 | tf_op jit(solution)/shard_map/while/body/eval_jaxpr/ppermute | solution.py:15
  250.8 20.4 %collective-permute-start.1 = (bf16[256,256]{1,0:T(8,128)(2,1)}, bf16[256,256]{1,0:T(8,128)(2,1)}, u32[]{:S(2)}, u32[]{:S(2)}) collective-permute-start(bf16[256,256]{1,0:T(8,128)(2,1)} %copy.228), channel_id=1, source_target_pairs={{0,4},{4,8},{8,12},{12,16},{16,20},{20,24},{24,28},{28,0},{1,5},{5... | collective-permute-start | bytes 393224 | tf_op jit(solution)/shard_map/while/body/eval_jaxpr/ppermute | solution.py:15
  257.5 2.6 copy-start
  261.2 7.7 %collective-permute-start.3 = (bf16[256,256]{0,1:T(8,128)(2,1)S(1)}, bf16[256,256]{0,1:T(8,128)(2,1)S(1)}, u32[]{:S(2)}, u32[]{:S(2)}) collective-permute-start(bf16[256,256]{0,1:T(8,128)(2,1)S(1)} %fusion.85), channel_id=1, source_target_pairs={{0,4},{4,8},{8,12},{12,16},{16,20},{20,24},{24,28},{28,0},{1,5},{5... | collective-permute-start | bytes 393224 | tf_op jit(solution)/shard_map/while/body/eval_jaxpr/ppermute | solution.py:15
  262.8 7.7 %collective-permute-start.2 = (bf16[256,256]{0,1:T(8,128)(2,1)S(1)}, bf16[256,256]{0,1:T(8,128)(2,1)S(1)}, u32[]{:S(2)}, u32[]{:S(2)}) collective-permute-start(bf16[256,256]{0,1:T(8,128)(2,1)S(1)} %fusion.84), channel_id=1, source_target_pairs={{0,4},{4,8},{8,12},{12,16},{16,20},{20,24},{24,28},{28,0},{1,5},{5... | collective-permute-start | bytes 393224 | tf_op jit(solution)/shard_map/while/body/eval_jaxpr/ppermute | solution.py:15
  272.8 23.7 %collective-permute-start = (bf16[256,256]{1,0:T(8,128)(2,1)}, bf16[256,256]{1,0:T(8,128)(2,1)}, u32[]{:S(2)}, u32[]{:S(2)}) collective-permute-start(bf16[256,256]{1,0:T(8,128)(2,1)} %copy.227), channel_id=1, source_target_pairs={{0,4},{4,8},{8,12},{12,16},{16,20},{20,24},{24,28},{28,0},{1,5},{5... | collective-permute-start | bytes 393224 | tf_op jit(solution)/shard_map/while/body/eval_jaxpr/ppermute | solution.py:15
  274.4 22.1 %collective-permute-start.1 = (bf16[256,256]{1,0:T(8,128)(2,1)}, bf16[256,256]{1,0:T(8,128)(2,1)}, u32[]{:S(2)}, u32[]{:S(2)}) collective-permute-start(bf16[256,256]{1,0:T(8,128)(2,1)} %copy.228), channel_id=1, source_target_pairs={{0,4},{4,8},{8,12},{12,16},{16,20},{20,24},{24,28},{28,0},{1,5},{5... | collective-permute-start | bytes 393224 | tf_op jit(solution)/shard_map/while/body/eval_jaxpr/ppermute | solution.py:15
  281.8 2.6 copy-start
  285.5 7.7 %collective-permute-start.3 = (bf16[256,256]{0,1:T(8,128)(2,1)S(1)}, bf16[256,256]{0,1:T(8,128)(2,1)S(1)}, u32[]{:S(2)}, u32[]{:S(2)}) collective-permute-start(bf16[256,256]{0,1:T(8,128)(2,1)S(1)} %fusion.85), channel_id=1, source_target_pairs={{0,4},{4,8},{8,12},{12,16},{16,20},{20,24},{24,28},{28,0},{1,5},{5... | collective-permute-start | bytes 393224 | tf_op jit(solution)/shard_map/while/body/eval_jaxpr/ppermute | solution.py:15
  288.0 7.7 %collective-permute-start.2 = (bf16[256,256]{0,1:T(8,128)(2,1)S(1)}, bf16[256,256]{0,1:T(8,128)(2,1)S(1)}, u32[]{:S(2)}, u32[]{:S(2)}) collective-permute-start(bf16[256,256]{0,1:T(8,128)(2,1)S(1)} %fusion.84), channel_id=1, source_target_pairs={{0,4},{4,8},{8,12},{12,16},{16,20},{20,24},{24,28},{28,0},{1,5},{5... | collective-permute-start | bytes 393224 | tf_op jit(solution)/shard_map/while/body/eval_jaxpr/ppermute | solution.py:15
  298.1 23.9 %collective-permute-start = (bf16[256,256]{1,0:T(8,128)(2,1)}, bf16[256,256]{1,0:T(8,128)(2,1)}, u32[]{:S(2)}, u32[]{:S(2)}) collective-permute-start(bf16[256,256]{1,0:T(8,128)(2,1)} %copy.227), channel_id=1, source_target_pairs={{0,4},{4,8},{8,12},{12,16},{16,20},{20,24},{24,28},{28,0},{1,5},{5... | collective-permute-start | bytes 393224 | tf_op jit(solution)/shard_map/while/body/eval_jaxpr/ppermute | solution.py:15
  299.6 22.3 %collective-permute-start.1 = (bf16[256,256]{1,0:T(8,128)(2,1)}, bf16[256,256]{1,0:T(8,128)(2,1)}, u32[]{:S(2)}, u32[]{:S(2)}) collective-permute-start(bf16[256,256]{1,0:T(8,128)(2,1)} %copy.228), channel_id=1, source_target_pairs={{0,4},{4,8},{8,12},{12,16},{16,20},{20,24},{24,28},{28,0},{1,5},{5... | collective-permute-start | bytes 393224 | tf_op jit(solution)/shard_map/while/body/eval_jaxpr/ppermute | solution.py:15
  306.0 2.6 copy-start
  309.7 7.7 %collective-permute-start.3 = (bf16[256,256]{0,1:T(8,128)(2,1)S(1)}, bf16[256,256]{0,1:T(8,128)(2,1)S(1)}, u32[]{:S(2)}, u32[]{:S(2)}) collective-permute-start(bf16[256,256]{0,1:T(8,128)(2,1)S(1)} %fusion.85), channel_id=1, source_target_pairs={{0,4},{4,8},{8,12},{12,16},{16,20},{20,24},{24,28},{28,0},{1,5},{5... | collective-permute-start | bytes 393224 | tf_op jit(solution)/shard_map/while/body/eval_jaxpr/ppermute | solution.py:15
  313.2 8.0 %collective-permute-start.2 = (bf16[256,256]{0,1:T(8,128)(2,1)S(1)}, bf16[256,256]{0,1:T(8,128)(2,1)S(1)}, u32[]{:S(2)}, u32[]{:S(2)}) collective-permute-start(bf16[256,256]{0,1:T(8,128)(2,1)S(1)} %fusion.84), channel_id=1, source_target_pairs={{0,4},{4,8},{8,12},{12,16},{16,20},{20,24},{24,28},{28,0},{1,5},{5... | collective-permute-start | bytes 393224 | tf_op jit(solution)/shard_map/while/body/eval_jaxpr/ppermute | solution.py:15
  323.5 26.3 %collective-permute-start = (bf16[256,256]{1,0:T(8,128)(2,1)}, bf16[256,256]{1,0:T(8,128)(2,1)}, u32[]{:S(2)}, u32[]{:S(2)}) collective-permute-start(bf16[256,256]{1,0:T(8,128)(2,1)} %copy.227), channel_id=1, source_target_pairs={{0,4},{4,8},{8,12},{12,16},{16,20},{20,24},{24,28},{28,0},{1,5},{5... | collective-permute-start | bytes 393224 | tf_op jit(solution)/shard_map/while/body/eval_jaxpr/ppermute | solution.py:15
  325.1 24.7 %collective-permute-start.1 = (bf16[256,256]{1,0:T(8,128)(2,1)}, bf16[256,256]{1,0:T(8,128)(2,1)}, u32[]{:S(2)}, u32[]{:S(2)}) collective-permute-start(bf16[256,256]{1,0:T(8,128)(2,1)} %copy.228), channel_id=1, source_target_pairs={{0,4},{4,8},{8,12},{12,16},{16,20},{20,24},{24,28},{28,0},{1,5},{5... | collective-permute-start | bytes 393224 | tf_op jit(solution)/shard_map/while/body/eval_jaxpr/ppermute | solution.py:15
  333.4 2.6 copy-start
  337.2 9.1 %collective-permute-start.3 = (bf16[256,256]{0,1:T(8,128)(2,1)S(1)}, bf16[256,256]{0,1:T(8,128)(2,1)S(1)}, u32[]{:S(2)}, u32[]{:S(2)}) collective-permute-start(bf16[256,256]{0,1:T(8,128)(2,1)S(1)} %fusion.85), channel_id=1, source_target_pairs={{0,4},{4,8},{8,12},{12,16},{16,20},{20,24},{24,28},{28,0},{1,5},{5... | collective-permute-start | bytes 393224 | tf_op jit(solution)/shard_map/while/body/eval_jaxpr/ppermute | solution.py:15
  338.8 10.2 %collective-permute-start.2 = (bf16[256,256]{0,1:T(8,128)(2,1)S(1)}, bf16[256,256]{0,1:T(8,128)(2,1)S(1)}, u32[]{:S(2)}, u32[]{:S(2)}) collective-permute-start(bf16[256,256]{0,1:T(8,128)(2,1)S(1)} %fusion.84), channel_id=1, source_target_pairs={{0,4},{4,8},{8,12},{12,16},{16,20},{20,24},{24,28},{28,0},{1,5},{5... | collective-permute-start | bytes 393224 | tf_op jit(solution)/shard_map/while/body/eval_jaxpr/ppermute | solution.py:15
  351.3 21.6 %collective-permute-start = (bf16[256,256]{1,0:T(8,128)(2,1)}, bf16[256,256]{1,0:T(8,128)(2,1)}, u32[]{:S(2)}, u32[]{:S(2)}) collective-permute-start(bf16[256,256]{1,0:T(8,128)(2,1)} %copy.227), channel_id=1, source_target_pairs={{0,4},{4,8},{8,12},{12,16},{16,20},{20,24},{24,28},{28,0},{1,5},{5... | collective-permute-start | bytes 393224 | tf_op jit(solution)/shard_map/while/body/eval_jaxpr/ppermute | solution.py:15
  352.9 20.1 %collective-permute-start.1 = (bf16[256,256]{1,0:T(8,128)(2,1)}, bf16[256,256]{1,0:T(8,128)(2,1)}, u32[]{:S(2)}, u32[]{:S(2)}) collective-permute-start(bf16[256,256]{1,0:T(8,128)(2,1)} %copy.228), channel_id=1, source_target_pairs={{0,4},{4,8},{8,12},{12,16},{16,20},{20,24},{24,28},{28,0},{1,5},{5... | collective-permute-start | bytes 393224 | tf_op jit(solution)/shard_map/while/body/eval_jaxpr/ppermute | solution.py:15
  358.9 2.6 copy-start
  362.7 8.1 %collective-permute-start.3 = (bf16[256,256]{0,1:T(8,128)(2,1)S(1)}, bf16[256,256]{0,1:T(8,128)(2,1)S(1)}, u32[]{:S(2)}, u32[]{:S(2)}) collective-permute-start(bf16[256,256]{0,1:T(8,128)(2,1)S(1)} %fusion.85), channel_id=1, source_target_pairs={{0,4},{4,8},{8,12},{12,16},{16,20},{20,24},{24,28},{28,0},{1,5},{5... | collective-permute-start | bytes 393224 | tf_op jit(solution)/shard_map/while/body/eval_jaxpr/ppermute | solution.py:15
  363.7 8.5 %collective-permute-start.2 = (bf16[256,256]{0,1:T(8,128)(2,1)S(1)}, bf16[256,256]{0,1:T(8,128)(2,1)S(1)}, u32[]{:S(2)}, u32[]{:S(2)}) collective-permute-start(bf16[256,256]{0,1:T(8,128)(2,1)S(1)} %fusion.84), channel_id=1, source_target_pairs={{0,4},{4,8},{8,12},{12,16},{16,20},{20,24},{24,28},{28,0},{1,5},{5... | collective-permute-start | bytes 393224 | tf_op jit(solution)/shard_map/while/body/eval_jaxpr/ppermute | solution.py:15
  374.5 24.0 %collective-permute-start = (bf16[256,256]{1,0:T(8,128)(2,1)}, bf16[256,256]{1,0:T(8,128)(2,1)}, u32[]{:S(2)}, u32[]{:S(2)}) collective-permute-start(bf16[256,256]{1,0:T(8,128)(2,1)} %copy.227), channel_id=1, source_target_pairs={{0,4},{4,8},{8,12},{12,16},{16,20},{20,24},{24,28},{28,0},{1,5},{5... | collective-permute-start | bytes 393224 | tf_op jit(solution)/shard_map/while/body/eval_jaxpr/ppermute | solution.py:15
  376.1 22.5 %collective-permute-start.1 = (bf16[256,256]{1,0:T(8,128)(2,1)}, bf16[256,256]{1,0:T(8,128)(2,1)}, u32[]{:S(2)}, u32[]{:S(2)}) collective-permute-start(bf16[256,256]{1,0:T(8,128)(2,1)} %copy.228), channel_id=1, source_target_pairs={{0,4},{4,8},{8,12},{12,16},{16,20},{20,24},{24,28},{28,0},{1,5},{5... | collective-permute-start | bytes 393224 | tf_op jit(solution)/shard_map/while/body/eval_jaxpr/ppermute | solution.py:15
  383.6 2.6 copy-start
  387.3 9.0 %collective-permute-start.3 = (bf16[256,256]{0,1:T(8,128)(2,1)S(1)}, bf16[256,256]{0,1:T(8,128)(2,1)S(1)}, u32[]{:S(2)}, u32[]{:S(2)}) collective-permute-start(bf16[256,256]{0,1:T(8,128)(2,1)S(1)} %fusion.85), channel_id=1, source_target_pairs={{0,4},{4,8},{8,12},{12,16},{16,20},{20,24},{24,28},{28,0},{1,5},{5... | collective-permute-start | bytes 393224 | tf_op jit(solution)/shard_map/while/body/eval_jaxpr/ppermute | solution.py:15
  389.0 8.8 %collective-permute-start.2 = (bf16[256,256]{0,1:T(8,128)(2,1)S(1)}, bf16[256,256]{0,1:T(8,128)(2,1)S(1)}, u32[]{:S(2)}, u32[]{:S(2)}) collective-permute-start(bf16[256,256]{0,1:T(8,128)(2,1)S(1)} %fusion.84), channel_id=1, source_target_pairs={{0,4},{4,8},{8,12},{12,16},{16,20},{20,24},{24,28},{28,0},{1,5},{5... | collective-permute-start | bytes 393224 | tf_op jit(solution)/shard_map/while/body/eval_jaxpr/ppermute | solution.py:15
  400.1 25.2 %collective-permute-start = (bf16[256,256]{1,0:T(8,128)(2,1)}, bf16[256,256]{1,0:T(8,128)(2,1)}, u32[]{:S(2)}, u32[]{:S(2)}) collective-permute-start(bf16[256,256]{1,0:T(8,128)(2,1)} %copy.227), channel_id=1, source_target_pairs={{0,4},{4,8},{8,12},{12,16},{16,20},{20,24},{24,28},{28,0},{1,5},{5... | collective-permute-start | bytes 393224 | tf_op jit(solution)/shard_map/while/body/eval_jaxpr/ppermute | solution.py:15
  401.7 23.6 %collective-permute-start.1 = (bf16[256,256]{1,0:T(8,128)(2,1)}, bf16[256,256]{1,0:T(8,128)(2,1)}, u32[]{:S(2)}, u32[]{:S(2)}) collective-permute-start(bf16[256,256]{1,0:T(8,128)(2,1)} %copy.228), channel_id=1, source_target_pairs={{0,4},{4,8},{8,12},{12,16},{16,20},{20,24},{24,28},{28,0},{1,5},{5... | collective-permute-start | bytes 393224 | tf_op jit(solution)/shard_map/while/body/eval_jaxpr/ppermute | solution.py:15
  410.1 2.6 copy-start
  413.8 9.0 %collective-permute-start.3 = (bf16[256,256]{0,1:T(8,128)(2,1)S(1)}, bf16[256,256]{0,1:T(8,128)(2,1)S(1)}, u32[]{:S(2)}, u32[]{:S(2)}) collective-permute-start(bf16[256,256]{0,1:T(8,128)(2,1)S(1)} %fusion.85), channel_id=1, source_target_pairs={{0,4},{4,8},{8,12},{12,16},{16,20},{20,24},{24,28},{28,0},{1,5},{5... | collective-permute-start | bytes 393224 | tf_op jit(solution)/shard_map/while/body/eval_jaxpr/ppermute | solution.py:15
  415.2 9.4 %collective-permute-start.2 = (bf16[256,256]{0,1:T(8,128)(2,1)S(1)}, bf16[256,256]{0,1:T(8,128)(2,1)S(1)}, u32[]{:S(2)}, u32[]{:S(2)}) collective-permute-start(bf16[256,256]{0,1:T(8,128)(2,1)S(1)} %fusion.84), channel_id=1, source_target_pairs={{0,4},{4,8},{8,12},{12,16},{16,20},{20,24},{24,28},{28,0},{1,5},{5... | collective-permute-start | bytes 393224 | tf_op jit(solution)/shard_map/while/body/eval_jaxpr/ppermute | solution.py:15
  426.5 11.6 %all-to-all-start.5 = ((bf16[8,64,256]{2,1,0:T(8,128)(2,1)}), bf16[8,64,256]{2,1,0:T(8,128)(2,1)S(1)}, u32[]{:S(2)}, u32[]{:S(2)}) async-start(bf16[8,64,256]{2,1,0:T(8,128)(2,1)} %copy.132), calls=%async_computation.5 | async-start | bytes 524288 | tf_op jit(solution)/shard_map/all_to_all | solution.py:240
  438.1 16.4 %all-to-all-start.4 = ((bf16[8,64,256]{2,1,0:T(8,128)(2,1)}), bf16[8,64,256]{2,1,0:T(8,128)(2,1)S(1)}, u32[]{:S(2)}, u32[]{:S(2)}) async-start(bf16[8,64,256]{2,1,0:T(8,128)(2,1)} %copy.127), calls=%async_computation.4 | async-start | bytes 524288 | tf_op jit(solution)/shard_map/all_to_all | solution.py:237
  441.8 16.3 %copy-start.7 = (s32[4]{0:T(128)S(1)}, s32[4]{0:T(128)}, u32[]{:S(2)}) copy-start(s32[4]{0:T(128)} %copy-done.6) | copy-start | bytes 52
  454.5 19.9 %all-to-all-start.3 = ((bf16[8,64,1024]{2,1,0:T(8,128)(2,1)}), bf16[8,64,1024]{2,1,0:T(8,128)(2,1)S(1)}, u32[]{:S(2)}, u32[]{:S(2)}) async-start(bf16[8,64,1024]{2,1,0:T(8,128)(2,1)} %copy.122), calls=%async_computation.3 | async-start | bytes 2097152 | tf_op jit(solution)/shard_map/all_to_all | solution.py:234
  458.0 88.7 %reduce-scatter.2.cloned.1.call-start = ((), (), s32[]{:S(2)}) async-start(), calls=%async_computation.10 | async-start | bytes 5242880 | tf_op jit(solution)/shard_map/reduce_scatter | solution.py:259
  494.2 6.1 %copy-start.3 = (bf16[8192,256]{1,0:T(8,128)(2,1)S(1)}, bf16[8192,256]{1,0:T(8,128)(2,1)}, u32[]{:S(2)}) copy-start(bf16[8192,256]{1,0:T(8,128)(2,1)} %param.18) | copy-start | bytes 12582916
  503.6 1.0 copy-start.4
  (2 other events, 1.9 us)
Sparse Core Ops, SparseCore 0:
  9.6 37.1 all-gather.3
  74.0 51.0 all-gather.7
  127.2 39.3 all-gather.5
  503.7 43.0 reduce-scatter.1
where the time goes:
time: 556 us; the launch traced here: 553 us
  waiting for transfers between devices  231 us (42%)
  matrix products  104 us (19%)
  local copies, waits for them, and re-layouts  90.9 us (16%)
  starting transfers between devices  56.4 us (10%)
  other arithmetic  49 us (9%)
  between operations  14.1 us (3%)
  loops' own time  8.15 us (1%)
    ppermute x32, waiting for transfers between devices, from_behind(): return lax.ppermute(value, axis, pairs)  53.3 us
    reduce_scatter x1, waiting for transfers between devices, per_device(): lax.psum_scatter(grad_terms.astype(jnp.bfloat16), 'heads', scatter_dimens...  40.6 us
    all_gather x1, waiting for transfers between devices, per_device(): piece = lax.all_gather(activations, 'heads', axis=1, tiled=True)  37.1 us
    all_gather x1, waiting for transfers between devices, per_device(): key_piece = lax.all_gather(ctx_k, 'ctx', axis=0, tiled=True)  36.9 us
    ppermute x32, starting transfers between devices, from_behind(): return lax.ppermute(value, axis, pairs)  30.5 us
    dot_general x3, matrix products, transposed_dot(): lax.dot_general(left, weight, (((1,), (1,)), ((), ())), preferred_element...  28.3 us
    all_to_all x1, waiting for transfers between devices, per_device(): lax.all_to_all(spread(send_map, loader_q, block_rows), 'ctx', split_axis=...  27.5 us
    while x16, local copies, waits for them, and re-layouts  25 us
  transfers between devices with their start and end apart: 42, of which 24 were waited for; matrix products, arithmetic and copies ran while one was open for 25% of the time, Pallas kernels for 0%

commit v1 on v0

--- a/solution.py
+++ b/solution.py
@@ -185,8 +185,11 @@
         return lax.fori_loop(0, rows // width, grads_one_block, (dquery, empty_rows, empty_rows))
 
     dq_start = jnp.zeros((tok_dev, groups, per_group, head_dim), jnp.float32)
-    key_piece = lax.all_gather(ctx_k, "ctx", axis=0, tiled=True)
-    value_piece = lax.all_gather(ctx_v, "ctx", axis=0, tiled=True)
+    key_piece, value_piece = jnp.split(
+        lax.all_gather(jnp.concatenate([ctx_k, ctx_v], axis=1), "ctx", axis=0, tiled=True),
+        [ctx_k.shape[1]],
+        axis=1,
+    )
     rows = key_piece.shape[0]
     width = math.gcd(rows, 512)
 

time: 556 us -> 539 us (0.969)
  waiting for transfers between devices: 231 us -> 209 us
    all_gather x2 -> x1, waiting for transfers between devices: 36.9 us -> 0.72 us  [per_device(): lax.all_gather(jnp.concatenate([ctx_k, ctx_v], axis=1), 'ctx', axis=0, ti...]
    all_to_all x1, waiting for transfers between devices: 0.01 us -> 7.48 us  [per_device(): lax.all_to_all(spread(send_map, loader_k, block_rows), 'ctx', split_axis=...]
    all_to_all x1, waiting for transfers between devices: 27.5 us -> 34.2 us  [per_device(): lax.all_to_all(spread(send_map, loader_q, block_rows), 'ctx', split_axis=...]
  transfers between devices with their start and end apart: 42 -> 41, of which waited for: 24 -> 25; matrix products, arithmetic and copies ran while one was open for 25% -> 26% of each run, Pallas kernels for 0% -> 0%
where the time goes in v1:
time: 539 us; the launch traced here: 536 us
  waiting for transfers between devices  209 us (39%)
  matrix products  104 us (19%)
  local copies, waits for them, and re-layouts  93.3 us (17%)
  starting transfers between devices  55 us (10%)
  other arithmetic  51.3 us (10%)
  between operations  14.1 us (3%)
  loops' own time  9.05 us (2%)
    ppermute x32, waiting for transfers between devices, from_behind(): return lax.ppermute(value, axis, pairs)  52.2 us
    reduce_scatter x1, waiting for transfers between devices, per_device(): lax.psum_scatter(grad_terms.astype(jnp.bfloat16), 'heads', scatter_dimens...  40.6 us
    all_gather x1, waiting for transfers between devices, per_device(): piece = lax.all_gather(activations, 'heads', axis=1, tiled=True)  37.5 us
    all_to_all x1, waiting for transfers between devices, per_device(): lax.all_to_all(spread(send_map, loader_q, block_rows), 'ctx', split_axis=...  34.2 us
    ppermute x32, starting transfers between devices, from_behind(): return lax.ppermute(value, axis, pairs)  30.3 us
    dot_general x3, matrix products, transposed_dot(): lax.dot_general(left, weight, (((1,), (1,)), ((), ())), preferred_element...  28.5 us
    while x16, local copies, waits for them, and re-layouts  25 us
    reduce_or x8, other arithmetic, grads_one_block(): dq_add, dk_blk, dv_blk = lax.cond(jnp.any(mask), one_run, skip, 0)  17 us
  transfers between devices with their start and end apart: 41, of which 25 were waited for; matrix products, arithmetic and copies ran while one was open for 26% of the time, Pallas kernels for 0%

profile of v1, /device:TPU:0, one launch (start us, length us, event | category | flops | bytes accessed | tf_op | source)
XLA Modules:
  0.0 535.7 jit_solution(4103943199858300213)
XLA Ops:
  9.3 37.5 %all-gather.3.cloned.1.call-done = bf16[256,8192]{1,0:T(8,128)(2,1)} async-done(((bf16[256,2048]{1,0:T(8,128)(2,1)}), bf16[256,8192]{1,0:T(8,128)(2,1)}) %all-gather.3.cloned.1.call-update) | async-done | bytes 4194320 | tf_op jit(solution)/shard_map/all_gather | solution.py:62
  46.8 4.7 convolution_convert_fusion.13
  52.6 5.5 %all-to-all-start.1 = ((bf16[8,64,256]{2,1,0:T(8,128)(2,1)}), bf16[8,64,256]{2,1,0:T(8,128)(2,1)S(1)}, u32[]{:S(2)}, u32[]{:S(2)}) async-start(bf16[8,64,256]{2,1,0:T(8,128)(2,1)} %copy.107), calls=%async_computation.1 | async-start | bytes 524288 | tf_op jit(solution)/shard_map/all_to_all | solution.py:83
  58.1 4.7 convolution_convert_fusion.14
  63.9 3.5 all-to-all-done.1
  67.4 3.6 all-to-all-start
  72.4 7.5 %all-to-all-done = bf16[8,64,256]{2,1,0:T(8,128)(2,1)S(1)} async-done(((bf16[8,64,256]{2,1,0:T(8,128)(2,1)}), bf16[8,64,256]{2,1,0:T(8,128)(2,1)S(1)}, u32[]{:S(2)}, u32[]{:S(2)}) %all-to-all-start) | async-done | bytes 262176 | tf_op jit(solution)/shard_map/all_to_all | solution.py:80
  82.6 11.7 %convolution_convert_fusion.4 = bf16[256,1024]{1,0:T(8,128)(2,1)S(1)} fusion(bf16[256,8192]{1,0:T(8,128)(2,1)} %all-gather.3.cloned.1.call-done, bf16[8192,1024]{1,0:T(8,128)(2,1)} %param.16), kind=kOutput, calls=%fused_computation.45 | convolution fusion | flops 4295229440 | bytes 21495808 | tf_op jit(solution)/shard_map/dot_general | solution.py:64
  96.5 3.7 all-to-all-start.2
  105.4 34.2 %all-to-all-done.2 = bf16[8,64,1024]{2,1,0:T(8,128)(2,1)S(1)} async-done(((bf16[8,64,1024]{2,1,0:T(8,128)(2,1)}), bf16[8,64,1024]{2,1,0:T(8,128)(2,1)S(1)}, u32[]{:S(2)}, u32[]{:S(2)}) %all-to-all-start.2) | async-done | bytes 1048608 | tf_op jit(solution)/shard_map/all_to_all | solution.py:77
  142.8 3.0 fusion.55
  147.3 2.3 copy.114
  150.7 47.5 %while.56 = (s32[]{:T(128)}, f32[2,4,256]{2,1,0:T(4,128)S(1)}, f32[2,4,256]{2,1,0:T(4,128)S(1)}, f32[2,4,256,128]{3,2,1,0:T(8,128)}, s32[256]{0:T(256)}, /*index...) while((s32[]{:T(128)}, f32[2,4,256]{2,1,0:T(4,128)S(1)}, ...), condition=%wide.region_10.11_spmd, body=%wide.region_4.10_spmd.sunk | while | flops 1892683776 | bytes 25835900 | solution.py:208
  154.4 8.2 %conditional.5 = ((f32[2,4,256]{2,1,0:T(4,128)S(1)}, f32[2,4,256]{2,1,0:T(4,128)S(1)}, f32[2,4,256,128]{3,2,1,0:T(8,128)})) conditional(s32[]{:T(128)} %convert_element_type.201, (f32[2,4,256]{2,1,0:T(4,128)S(1)}, f32[2,4,256]{2,1,0:T(4,128)S(1)}, f32[2,4,256,128]{3,2,1,0:T(8,128)}) %tuple.117, (pred[256,512]{0,1:T(8,128)(4,1)S(1)}, ...), branch_computations={%region_6.6_spmd, %region_7.9_spmd} | conditional | flops 1892159488 | bytes 25690204 | solution.py:126
  157.4 4.2 fusion.8
  166.3 8.2 %conditional.5 = ((f32[2,4,256]{2,1,0:T(4,128)S(1)}, f32[2,4,256]{2,1,0:T(4,128)S(1)}, f32[2,4,256,128]{3,2,1,0:T(8,128)})) conditional(s32[]{:T(128)} %convert_element_type.201, (f32[2,4,256]{2,1,0:T(4,128)S(1)}, f32[2,4,256]{2,1,0:T(4,128)S(1)}, f32[2,4,256,128]{3,2,1,0:T(8,128)}) %tuple.117, (pred[256,512]{0,1:T(8,128)(4,1)S(1)}, ...), branch_computations={%region_6.6_spmd, %region_7.9_spmd} | conditional | flops 1892159488 | bytes 25690204 | solution.py:126
  169.2 4.2 fusion.8
  178.1 8.2 %conditional.5 = ((f32[2,4,256]{2,1,0:T(4,128)S(1)}, f32[2,4,256]{2,1,0:T(4,128)S(1)}, f32[2,4,256,128]{3,2,1,0:T(8,128)})) conditional(s32[]{:T(128)} %convert_element_type.201, (f32[2,4,256]{2,1,0:T(4,128)S(1)}, f32[2,4,256]{2,1,0:T(4,128)S(1)}, f32[2,4,256,128]{3,2,1,0:T(8,128)}) %tuple.117, (pred[256,512]{0,1:T(8,128)(4,1)S(1)}, ...), branch_computations={%region_6.6_spmd, %region_7.9_spmd} | conditional | flops 1892159488 | bytes 25690204 | solution.py:126
  181.1 4.2 fusion.8
  190.0 8.2 %conditional.5 = ((f32[2,4,256]{2,1,0:T(4,128)S(1)}, f32[2,4,256]{2,1,0:T(4,128)S(1)}, f32[2,4,256,128]{3,2,1,0:T(8,128)})) conditional(s32[]{:T(128)} %convert_element_type.201, (f32[2,4,256]{2,1,0:T(4,128)S(1)}, f32[2,4,256]{2,1,0:T(4,128)S(1)}, f32[2,4,256,128]{3,2,1,0:T(8,128)}) %tuple.117, (pred[256,512]{0,1:T(8,128)(4,1)S(1)}, ...), branch_computations={%region_6.6_spmd, %region_7.9_spmd} | conditional | flops 1892159488 | bytes 25690204 | solution.py:126
  193.0 4.2 fusion.8
  198.2 2.7 fusion.51
  203.2 202.7 %while.57 = (s32[]{:T(128)}, f32[256,2,4,128]{3,0,2,1:T(8,128)S(1)}, bf16[256,256]{1,0:T(8,128)(2,1)}, bf16[256,256]{1,0:T(8,128)(2,1)}, f32[256,256]{0,1:T(8,12...) while((s32[]{:T(128)}, ...), condition=%wide.region_15.16_spmd.clone, body=%wide.region_11.15_spmd.clone.sunk | while | flops 676593664 | bytes 24142468 | solution.py:229
  209.5 2.1 fusion.84
  212.3 5.6 %conditional.6 = (f32[256,2,4,128]{3,0,2,1:T(8,128)S(1)}, f32[256,256]{0,1:T(8,128)S(1)}, f32[256,256]{0,1:T(8,128)S(1)}) conditional(s32[]{:T(128)} %convert_element_type.204, () %tuple.121, (pred[256,256]{0,1:T(8,128)(4,1)}, bf16[256,256]{1,0:T(8,128)(2,1)}, bf16[256,2,4,128]{0,3,2,1:T(8,128)(2,1)}, f32[2,4,256]{2,1,0:T(4,128)}, ...), branch_computations={%region_13.13_spmd, %region_14.14_spmd} | conditional | flops 675282944 | bytes 16203828 | solution.py:179
  218.0 2.8 collective-permute-start.3
  221.2 5.9 %collective-permute-done.3 = bf16[256,256]{0,1:T(8,128)(2,1)S(1)} collective-permute-done((bf16[256,256]{0,1:T(8,128)(2,1)S(1)}, bf16[256,256]{0,1:T(8,128)(2,1)S(1)}, u32[]{:S(2)}, u32[]{:S(2)}) %collective-permute-start.3) | collective-permute-done | bytes 131104 | tf_op jit(solution)/shard_map/while/body/eval_jaxpr/ppermute | solution.py:15
  234.2 2.1 fusion.84
  236.9 5.6 %conditional.6 = (f32[256,2,4,128]{3,0,2,1:T(8,128)S(1)}, f32[256,256]{0,1:T(8,128)S(1)}, f32[256,256]{0,1:T(8,128)S(1)}) conditional(s32[]{:T(128)} %convert_element_type.204, () %tuple.121, (pred[256,256]{0,1:T(8,128)(4,1)}, bf16[256,256]{1,0:T(8,128)(2,1)}, bf16[256,2,4,128]{0,3,2,1:T(8,128)(2,1)}, f32[2,4,256]{2,1,0:T(4,128)}, ...), branch_computations={%region_13.13_spmd, %region_14.14_spmd} | conditional | flops 675282944 | bytes 16203828 | solution.py:179
  244.6 2.5 collective-permute-start.2
  247.5 3.4 collective-permute-done.3
  258.8 2.1 fusion.84
  261.6 5.6 %conditional.6 = (f32[256,2,4,128]{3,0,2,1:T(8,128)S(1)}, f32[256,256]{0,1:T(8,128)S(1)}, f32[256,256]{0,1:T(8,128)S(1)}) conditional(s32[]{:T(128)} %convert_element_type.204, () %tuple.121, (pred[256,256]{0,1:T(8,128)(4,1)}, bf16[256,256]{1,0:T(8,128)(2,1)}, bf16[256,2,4,128]{0,3,2,1:T(8,128)(2,1)}, f32[2,4,256]{2,1,0:T(4,128)}, ...), branch_computations={%region_13.13_spmd, %region_14.14_spmd} | conditional | flops 675282944 | bytes 16203828 | solution.py:179
  267.2 2.4 collective-permute-start.3
  272.4 2.5 collective-permute-done.3
  274.9 3.4 collective-permute-done.2
  283.7 2.1 fusion.84
  286.5 5.6 %conditional.6 = (f32[256,2,4,128]{3,0,2,1:T(8,128)S(1)}, f32[256,256]{0,1:T(8,128)S(1)}, f32[256,256]{0,1:T(8,128)S(1)}) conditional(s32[]{:T(128)} %convert_element_type.204, () %tuple.121, (pred[256,256]{0,1:T(8,128)(4,1)}, bf16[256,256]{1,0:T(8,128)(2,1)}, bf16[256,2,4,128]{0,3,2,1:T(8,128)(2,1)}, f32[2,4,256]{2,1,0:T(4,128)}, ...), branch_computations={%region_13.13_spmd, %region_14.14_spmd} | conditional | flops 675282944 | bytes 16203828 | solution.py:179
  296.5 3.3 collective-permute-done.3
  299.8 2.8 collective-permute-done.2
  309.1 2.1 fusion.84
  311.9 5.6 %conditional.6 = (f32[256,2,4,128]{3,0,2,1:T(8,128)S(1)}, f32[256,256]{0,1:T(8,128)S(1)}, f32[256,256]{0,1:T(8,128)S(1)}) conditional(s32[]{:T(128)} %convert_element_type.204, () %tuple.121, (pred[256,256]{0,1:T(8,128)(4,1)}, bf16[256,256]{1,0:T(8,128)(2,1)}, bf16[256,2,4,128]{0,3,2,1:T(8,128)(2,1)}, f32[2,4,256]{2,1,0:T(4,128)}, ...), branch_computations={%region_13.13_spmd, %region_14.14_spmd} | conditional | flops 675282944 | bytes 16203828 | solution.py:179
  319.3 5.9 %collective-permute-done.3 = bf16[256,256]{0,1:T(8,128)(2,1)S(1)} collective-permute-done((bf16[256,256]{0,1:T(8,128)(2,1)S(1)}, bf16[256,256]{0,1:T(8,128)(2,1)S(1)}, u32[]{:S(2)}, u32[]{:S(2)}) %collective-permute-start.3) | collective-permute-done | bytes 131104 | tf_op jit(solution)/shard_map/while/body/eval_jaxpr/ppermute | solution.py:15
  332.0 3.4 collective-permute-start.1
  336.9 2.1 fusion.84
  339.6 5.6 %conditional.6 = (f32[256,2,4,128]{3,0,2,1:T(8,128)S(1)}, f32[256,256]{0,1:T(8,128)S(1)}, f32[256,256]{0,1:T(8,128)S(1)}) conditional(s32[]{:T(128)} %convert_element_type.204, () %tuple.121, (pred[256,256]{0,1:T(8,128)(4,1)}, bf16[256,256]{1,0:T(8,128)(2,1)}, bf16[256,2,4,128]{0,3,2,1:T(8,128)(2,1)}, f32[2,4,256]{2,1,0:T(4,128)}, ...), branch_computations={%region_13.13_spmd, %region_14.14_spmd} | conditional | flops 675282944 | bytes 16203828 | solution.py:179
  346.7 2.2 collective-permute-start.2
  349.2 5.1 collective-permute-done.3
  364.7 5.6 %conditional.6 = (f32[256,2,4,128]{3,0,2,1:T(8,128)S(1)}, f32[256,256]{0,1:T(8,128)S(1)}, f32[256,256]{0,1:T(8,128)S(1)}) conditional(s32[]{:T(128)} %convert_element_type.204, () %tuple.121, (pred[256,256]{0,1:T(8,128)(4,1)}, bf16[256,256]{1,0:T(8,128)(2,1)}, bf16[256,2,4,128]{0,3,2,1:T(8,128)(2,1)}, f32[2,4,256]{2,1,0:T(4,128)}, ...), branch_computations={%region_13.13_spmd, %region_14.14_spmd} | conditional | flops 675282944 | bytes 16203828 | solution.py:179
  373.1 6.3 %collective-permute-done.3 = bf16[256,256]{0,1:T(8,128)(2,1)S(1)} collective-permute-done((bf16[256,256]{0,1:T(8,128)(2,1)S(1)}, bf16[256,256]{0,1:T(8,128)(2,1)S(1)}, u32[]{:S(2)}, u32[]{:S(2)}) %collective-permute-start.3) | collective-permute-done | bytes 131104 | tf_op jit(solution)/shard_map/while/body/eval_jaxpr/ppermute | solution.py:15
  389.4 5.6 %conditional.6 = (f32[256,2,4,128]{3,0,2,1:T(8,128)S(1)}, f32[256,256]{0,1:T(8,128)S(1)}, f32[256,256]{0,1:T(8,128)S(1)}) conditional(s32[]{:T(128)} %convert_element_type.204, () %tuple.121, (pred[256,256]{0,1:T(8,128)(4,1)}, bf16[256,256]{1,0:T(8,128)(2,1)}, bf16[256,2,4,128]{0,3,2,1:T(8,128)(2,1)}, f32[2,4,256]{2,1,0:T(4,128)}, ...), branch_computations={%region_13.13_spmd, %region_14.14_spmd} | conditional | flops 675282944 | bytes 16203828 | solution.py:179
  396.1 2.9 collective-permute-start.2
  399.3 3.6 collective-permute-done.3
  403.0 2.2 collective-permute-done.2
  407.1 4.8 all-to-all-start.5
  414.1 6.1 %all-to-all-done.5 = bf16[8,64,256]{2,1,0:T(8,128)(2,1)S(1)} async-done(((bf16[8,64,256]{2,1,0:T(8,128)(2,1)}), bf16[8,64,256]{2,1,0:T(8,128)(2,1)S(1)}, u32[]{:S(2)}, u32[]{:S(2)}) %all-to-all-start.5) | async-done | bytes 262176 | tf_op jit(solution)/shard_map/all_to_all | solution.py:243
  420.1 3.4 all-to-all-start.4
  426.6 10.0 %all-to-all-done.4 = bf16[8,64,256]{2,1,0:T(8,128)(2,1)S(1)} async-done(((bf16[8,64,256]{2,1,0:T(8,128)(2,1)}), bf16[8,64,256]{2,1,0:T(8,128)(2,1)S(1)}, u32[]{:S(2)}, u32[]{:S(2)}) %all-to-all-start.4) | async-done | bytes 262176 | tf_op jit(solution)/shard_map/all_to_all | solution.py:240
  436.6 3.6 all-to-all-start.3
  440.9 15.6 %all-to-all-done.3 = bf16[8,64,1024]{2,1,0:T(8,128)(2,1)S(1)} async-done(((bf16[8,64,1024]{2,1,0:T(8,128)(2,1)}), bf16[8,64,1024]{2,1,0:T(8,128)(2,1)S(1)}, u32[]{:S(2)}, u32[]{:S(2)}) %all-to-all-start.3) | async-done | bytes 1048608 | tf_op jit(solution)/shard_map/all_to_all | solution.py:237
  457.5 19.1 %fusion.57 = f32[256,8192]{1,0:T(8,128)} fusion(bf16[256,1024]{1,0:T(8,128)(2,1)S(1)} %bitcast.128, bf16[8192,1024]{1,0:T(8,128)(2,1)} %param.16), kind=kOutput, calls=%fused_computation.93 | convolution fusion | flops 4294967296 | bytes 25690112 | tf_op jit(solution)/shard_map/dot_general | solution.py:43
  476.6 6.1 %convolution_add_fusion.1 = f32[256,8192]{1,0:T(8,128)S(1)} fusion(f32[256,8192]{1,0:T(8,128)} %fusion.57, bf16[256,256]{1,0:T(8,128)(2,1)S(1)} %bitcast.133, bf16[8192,256]{1,0:T(8,128)(2,1)} %param.17), kind=kOutput, calls=%fused_computation.39 | convolution fusion | flops 1075838976 | bytes 21102592 | tf_op jit(solution)/shard_map/dot_general | solution.py:43
  482.7 3.3 fusion.24
  488.6 40.6 %reduce-scatter.2.cloned.1.call-done = bf16[256,2048]{1,0:T(8,128)(2,1)} async-done(((bf16[256,8192]{1,0:T(8,128)(2,1)}), bf16[256,2048]{1,0:T(8,128)(2,1)}) %reduce-scatter.2.cloned.1.call-update) | async-done | bytes 1048592 | tf_op jit(solution)/shard_map/reduce_scatter | solution.py:262
  (326 shorter events, 185.2 us)
Async XLA Ops:
  7.2 39.6 %all-gather.3.cloned.1.call-start = ((), (), s32[]{:S(2)}) async-start(), calls=%async_computation.7 | async-start | bytes 5242880 | tf_op jit(solution)/shard_map/all_gather | solution.py:62
  8.6 85.7 %copy-start.6 = (s32[4]{0:T(128)}, s32[4]{0:T(128)S(1)}, u32[]{:S(2)}) copy-start(s32[4]{0:T(128)S(1)} %dynamic_slice.75) | copy-start | bytes 52
  52.6 14.8 %all-to-all-start.1 = ((bf16[8,64,256]{2,1,0:T(8,128)(2,1)}), bf16[8,64,256]{2,1,0:T(8,128)(2,1)S(1)}, u32[]{:S(2)}, u32[]{:S(2)}) async-start(bf16[8,64,256]{2,1,0:T(8,128)(2,1)} %copy.107), calls=%async_computation.1 | async-start | bytes 524288 | tf_op jit(solution)/shard_map/all_to_all | solution.py:83
  67.4 12.5 %all-to-all-start = ((bf16[8,64,256]{2,1,0:T(8,128)(2,1)}), bf16[8,64,256]{2,1,0:T(8,128)(2,1)S(1)}, u32[]{:S(2)}, u32[]{:S(2)}) async-start(bf16[8,64,256]{2,1,0:T(8,128)(2,1)} %copy.103), calls=%async_computation | async-start | bytes 524288 | tf_op jit(solution)/shard_map/all_to_all | solution.py:80
  71.0 71.8 %all-gather.5.cloned.1.call-start = ((), (), s32[]{:S(2)}) async-start(), calls=%async_computation.8 | async-start | bytes 2359296 | tf_op jit(solution)/shard_map/all_gather | solution.py:189
  71.4 68.2 %copy-start.8 = (s32[4]{0:T(128)}, s32[4]{0:T(128)S(1)}, u32[]{:S(2)}) copy-start(s32[4]{0:T(128)S(1)} %and_select_fusion) | copy-start | bytes 52
  94.3 6.0 %copy-start.10 = (s32[8]{0:T(128)S(1)}, s32[8]{0:T(128)}, u32[]{:S(2)}) copy-start(s32[8]{0:T(128)} %param.19) | copy-start | bytes 100
  94.3 10.9 %copy-start.5 = (bf16[256,1024]{1,0:T(8,128)(2,1)S(1)}, bf16[256,1024]{1,0:T(8,128)(2,1)}, u32[]{:S(2)}) copy-start(bf16[256,1024]{1,0:T(8,128)(2,1)} %param.21) | copy-start | bytes 1572868
  96.5 43.1 %all-to-all-start.2 = ((bf16[8,64,1024]{2,1,0:T(8,128)(2,1)}), bf16[8,64,1024]{2,1,0:T(8,128)(2,1)S(1)}, u32[]{:S(2)}, u32[]{:S(2)}) async-start(bf16[8,64,1024]{2,1,0:T(8,128)(2,1)} %copy.111), calls=%async_computation.2 | async-start | bytes 2097152 | tf_op jit(solution)/shard_map/all_to_all | solution.py:77
  155.4 2.0 copy-start.1
  161.6 1.0 copy-start.2
  167.3 2.0 copy-start.1
  173.5 1.0 copy-start.2
  179.2 2.0 copy-start.1
  185.3 1.0 copy-start.2
  191.0 2.0 copy-start.1
  203.2 202.8 %copy-start.9 = (s32[4]{0:T(128)S(1)}, s32[4]{0:T(128)}, u32[]{:S(2)}) copy-start(s32[4]{0:T(128)} %copy-done.8) | copy-start | bytes 52
  205.0 24.4 %collective-permute-start = (bf16[256,256]{1,0:T(8,128)(2,1)}, bf16[256,256]{1,0:T(8,128)(2,1)}, u32[]{:S(2)}, u32[]{:S(2)}) collective-permute-start(bf16[256,256]{1,0:T(8,128)(2,1)} %copy.227), channel_id=1, source_target_pairs={{0,4},{4,8},{8,12},{12,16},{16,20},{20,24},{24,28},{28,0},{1,5},{5... | collective-permute-start | bytes 393224 | tf_op jit(solution)/shard_map/while/body/eval_jaxpr/ppermute | solution.py:15
  208.1 21.4 %collective-permute-start.1 = (bf16[256,256]{1,0:T(8,128)(2,1)}, bf16[256,256]{1,0:T(8,128)(2,1)}, u32[]{:S(2)}, u32[]{:S(2)}) collective-permute-start(bf16[256,256]{1,0:T(8,128)(2,1)} %copy.228), channel_id=1, source_target_pairs={{0,4},{4,8},{8,12},{12,16},{16,20},{20,24},{24,28},{28,0},{1,5},{5... | collective-permute-start | bytes 393224 | tf_op jit(solution)/shard_map/while/body/eval_jaxpr/ppermute | solution.py:15
  214.2 2.7 copy-start
  218.0 9.1 %collective-permute-start.3 = (bf16[256,256]{0,1:T(8,128)(2,1)S(1)}, bf16[256,256]{0,1:T(8,128)(2,1)S(1)}, u32[]{:S(2)}, u32[]{:S(2)}) collective-permute-start(bf16[256,256]{0,1:T(8,128)(2,1)S(1)} %fusion.86), channel_id=1, source_target_pairs={{0,4},{4,8},{8,12},{12,16},{16,20},{20,24},{24,28},{28,0},{1,5},{5... | collective-permute-start | bytes 393224 | tf_op jit(solution)/shard_map/while/body/eval_jaxpr/ppermute | solution.py:15
  220.8 7.9 %collective-permute-start.2 = (bf16[256,256]{0,1:T(8,128)(2,1)S(1)}, bf16[256,256]{0,1:T(8,128)(2,1)S(1)}, u32[]{:S(2)}, u32[]{:S(2)}) collective-permute-start(bf16[256,256]{0,1:T(8,128)(2,1)S(1)} %fusion.85), channel_id=1, source_target_pairs={{0,4},{4,8},{8,12},{12,16},{16,20},{20,24},{24,28},{28,0},{1,5},{5... | collective-permute-start | bytes 393224 | tf_op jit(solution)/shard_map/while/body/eval_jaxpr/ppermute | solution.py:15
  231.0 22.1 %collective-permute-start = (bf16[256,256]{1,0:T(8,128)(2,1)}, bf16[256,256]{1,0:T(8,128)(2,1)}, u32[]{:S(2)}, u32[]{:S(2)}) collective-permute-start(bf16[256,256]{1,0:T(8,128)(2,1)} %copy.227), channel_id=1, source_target_pairs={{0,4},{4,8},{8,12},{12,16},{16,20},{20,24},{24,28},{28,0},{1,5},{5... | collective-permute-start | bytes 393224 | tf_op jit(solution)/shard_map/while/body/eval_jaxpr/ppermute | solution.py:15
  232.6 20.5 %collective-permute-start.1 = (bf16[256,256]{1,0:T(8,128)(2,1)}, bf16[256,256]{1,0:T(8,128)(2,1)}, u32[]{:S(2)}, u32[]{:S(2)}) collective-permute-start(bf16[256,256]{1,0:T(8,128)(2,1)} %copy.228), channel_id=1, source_target_pairs={{0,4},{4,8},{8,12},{12,16},{16,20},{20,24},{24,28},{28,0},{1,5},{5... | collective-permute-start | bytes 393224 | tf_op jit(solution)/shard_map/while/body/eval_jaxpr/ppermute | solution.py:15
  238.9 2.6 copy-start
  242.6 8.4 %collective-permute-start.3 = (bf16[256,256]{0,1:T(8,128)(2,1)S(1)}, bf16[256,256]{0,1:T(8,128)(2,1)S(1)}, u32[]{:S(2)}, u32[]{:S(2)}) collective-permute-start(bf16[256,256]{0,1:T(8,128)(2,1)S(1)} %fusion.86), channel_id=1, source_target_pairs={{0,4},{4,8},{8,12},{12,16},{16,20},{20,24},{24,28},{28,0},{1,5},{5... | collective-permute-start | bytes 393224 | tf_op jit(solution)/shard_map/while/body/eval_jaxpr/ppermute | solution.py:15
  244.6 7.7 %collective-permute-start.2 = (bf16[256,256]{0,1:T(8,128)(2,1)S(1)}, bf16[256,256]{0,1:T(8,128)(2,1)S(1)}, u32[]{:S(2)}, u32[]{:S(2)}) collective-permute-start(bf16[256,256]{0,1:T(8,128)(2,1)S(1)} %fusion.85), channel_id=1, source_target_pairs={{0,4},{4,8},{8,12},{12,16},{16,20},{20,24},{24,28},{28,0},{1,5},{5... | collective-permute-start | bytes 393224 | tf_op jit(solution)/shard_map/while/body/eval_jaxpr/ppermute | solution.py:15
  254.7 24.4 %collective-permute-start = (bf16[256,256]{1,0:T(8,128)(2,1)}, bf16[256,256]{1,0:T(8,128)(2,1)}, u32[]{:S(2)}, u32[]{:S(2)}) collective-permute-start(bf16[256,256]{1,0:T(8,128)(2,1)} %copy.227), channel_id=1, source_target_pairs={{0,4},{4,8},{8,12},{12,16},{16,20},{20,24},{24,28},{28,0},{1,5},{5... | collective-permute-start | bytes 393224 | tf_op jit(solution)/shard_map/while/body/eval_jaxpr/ppermute | solution.py:15
  256.2 22.8 %collective-permute-start.1 = (bf16[256,256]{1,0:T(8,128)(2,1)}, bf16[256,256]{1,0:T(8,128)(2,1)}, u32[]{:S(2)}, u32[]{:S(2)}) collective-permute-start(bf16[256,256]{1,0:T(8,128)(2,1)} %copy.228), channel_id=1, source_target_pairs={{0,4},{4,8},{8,12},{12,16},{16,20},{20,24},{24,28},{28,0},{1,5},{5... | collective-permute-start | bytes 393224 | tf_op jit(solution)/shard_map/while/body/eval_jaxpr/ppermute | solution.py:15
  263.5 2.6 copy-start
  267.2 7.7 %collective-permute-start.3 = (bf16[256,256]{0,1:T(8,128)(2,1)S(1)}, bf16[256,256]{0,1:T(8,128)(2,1)S(1)}, u32[]{:S(2)}, u32[]{:S(2)}) collective-permute-start(bf16[256,256]{0,1:T(8,128)(2,1)S(1)} %fusion.86), channel_id=1, source_target_pairs={{0,4},{4,8},{8,12},{12,16},{16,20},{20,24},{24,28},{28,0},{1,5},{5... | collective-permute-start | bytes 393224 | tf_op jit(solution)/shard_map/while/body/eval_jaxpr/ppermute | solution.py:15
  270.6 7.7 %collective-permute-start.2 = (bf16[256,256]{0,1:T(8,128)(2,1)S(1)}, bf16[256,256]{0,1:T(8,128)(2,1)S(1)}, u32[]{:S(2)}, u32[]{:S(2)}) collective-permute-start(bf16[256,256]{0,1:T(8,128)(2,1)S(1)} %fusion.85), channel_id=1, source_target_pairs={{0,4},{4,8},{8,12},{12,16},{16,20},{20,24},{24,28},{28,0},{1,5},{5... | collective-permute-start | bytes 393224 | tf_op jit(solution)/shard_map/while/body/eval_jaxpr/ppermute | solution.py:15
  280.6 22.7 %collective-permute-start = (bf16[256,256]{1,0:T(8,128)(2,1)}, bf16[256,256]{1,0:T(8,128)(2,1)}, u32[]{:S(2)}, u32[]{:S(2)}) collective-permute-start(bf16[256,256]{1,0:T(8,128)(2,1)} %copy.227), channel_id=1, source_target_pairs={{0,4},{4,8},{8,12},{12,16},{16,20},{20,24},{24,28},{28,0},{1,5},{5... | collective-permute-start | bytes 393224 | tf_op jit(solution)/shard_map/while/body/eval_jaxpr/ppermute | solution.py:15
  282.2 21.2 %collective-permute-start.1 = (bf16[256,256]{1,0:T(8,128)(2,1)}, bf16[256,256]{1,0:T(8,128)(2,1)}, u32[]{:S(2)}, u32[]{:S(2)}) collective-permute-start(bf16[256,256]{1,0:T(8,128)(2,1)} %copy.228), channel_id=1, source_target_pairs={{0,4},{4,8},{8,12},{12,16},{16,20},{20,24},{24,28},{28,0},{1,5},{5... | collective-permute-start | bytes 393224 | tf_op jit(solution)/shard_map/while/body/eval_jaxpr/ppermute | solution.py:15
  288.4 2.6 copy-start
  292.1 7.7 %collective-permute-start.3 = (bf16[256,256]{0,1:T(8,128)(2,1)S(1)}, bf16[256,256]{0,1:T(8,128)(2,1)S(1)}, u32[]{:S(2)}, u32[]{:S(2)}) collective-permute-start(bf16[256,256]{0,1:T(8,128)(2,1)S(1)} %fusion.86), channel_id=1, source_target_pairs={{0,4},{4,8},{8,12},{12,16},{16,20},{20,24},{24,28},{28,0},{1,5},{5... | collective-permute-start | bytes 393224 | tf_op jit(solution)/shard_map/while/body/eval_jaxpr/ppermute | solution.py:15
  294.9 7.7 %collective-permute-start.2 = (bf16[256,256]{0,1:T(8,128)(2,1)S(1)}, bf16[256,256]{0,1:T(8,128)(2,1)S(1)}, u32[]{:S(2)}, u32[]{:S(2)}) collective-permute-start(bf16[256,256]{0,1:T(8,128)(2,1)S(1)} %fusion.85), channel_id=1, source_target_pairs={{0,4},{4,8},{8,12},{12,16},{16,20},{20,24},{24,28},{28,0},{1,5},{5... | collective-permute-start | bytes 393224 | tf_op jit(solution)/shard_map/while/body/eval_jaxpr/ppermute | solution.py:15
  304.9 22.4 %collective-permute-start = (bf16[256,256]{1,0:T(8,128)(2,1)}, bf16[256,256]{1,0:T(8,128)(2,1)}, u32[]{:S(2)}, u32[]{:S(2)}) collective-permute-start(bf16[256,256]{1,0:T(8,128)(2,1)} %copy.227), channel_id=1, source_target_pairs={{0,4},{4,8},{8,12},{12,16},{16,20},{20,24},{24,28},{28,0},{1,5},{5... | collective-permute-start | bytes 393224 | tf_op jit(solution)/shard_map/while/body/eval_jaxpr/ppermute | solution.py:15
  306.5 20.9 %collective-permute-start.1 = (bf16[256,256]{1,0:T(8,128)(2,1)}, bf16[256,256]{1,0:T(8,128)(2,1)}, u32[]{:S(2)}, u32[]{:S(2)}) collective-permute-start(bf16[256,256]{1,0:T(8,128)(2,1)} %copy.228), channel_id=1, source_target_pairs={{0,4},{4,8},{8,12},{12,16},{16,20},{20,24},{24,28},{28,0},{1,5},{5... | collective-permute-start | bytes 393224 | tf_op jit(solution)/shard_map/while/body/eval_jaxpr/ppermute | solution.py:15
  313.8 2.6 copy-start
  317.5 7.7 %collective-permute-start.3 = (bf16[256,256]{0,1:T(8,128)(2,1)S(1)}, bf16[256,256]{0,1:T(8,128)(2,1)S(1)}, u32[]{:S(2)}, u32[]{:S(2)}) collective-permute-start(bf16[256,256]{0,1:T(8,128)(2,1)S(1)} %fusion.86), channel_id=1, source_target_pairs={{0,4},{4,8},{8,12},{12,16},{16,20},{20,24},{24,28},{28,0},{1,5},{5... | collective-permute-start | bytes 393224 | tf_op jit(solution)/shard_map/while/body/eval_jaxpr/ppermute | solution.py:15
  318.9 7.7 %collective-permute-start.2 = (bf16[256,256]{0,1:T(8,128)(2,1)S(1)}, bf16[256,256]{0,1:T(8,128)(2,1)S(1)}, u32[]{:S(2)}, u32[]{:S(2)}) collective-permute-start(bf16[256,256]{0,1:T(8,128)(2,1)S(1)} %fusion.85), channel_id=1, source_target_pairs={{0,4},{4,8},{8,12},{12,16},{16,20},{20,24},{24,28},{28,0},{1,5},{5... | collective-permute-start | bytes 393224 | tf_op jit(solution)/shard_map/while/body/eval_jaxpr/ppermute | solution.py:15
  328.9 27.8 %collective-permute-start = (bf16[256,256]{1,0:T(8,128)(2,1)}, bf16[256,256]{1,0:T(8,128)(2,1)}, u32[]{:S(2)}, u32[]{:S(2)}) collective-permute-start(bf16[256,256]{1,0:T(8,128)(2,1)} %copy.227), channel_id=1, source_target_pairs={{0,4},{4,8},{8,12},{12,16},{16,20},{20,24},{24,28},{28,0},{1,5},{5... | collective-permute-start | bytes 393224 | tf_op jit(solution)/shard_map/while/body/eval_jaxpr/ppermute | solution.py:15
  332.0 24.7 %collective-permute-start.1 = (bf16[256,256]{1,0:T(8,128)(2,1)}, bf16[256,256]{1,0:T(8,128)(2,1)}, u32[]{:S(2)}, u32[]{:S(2)}) collective-permute-start(bf16[256,256]{1,0:T(8,128)(2,1)} %copy.228), channel_id=1, source_target_pairs={{0,4},{4,8},{8,12},{12,16},{16,20},{20,24},{24,28},{28,0},{1,5},{5... | collective-permute-start | bytes 393224 | tf_op jit(solution)/shard_map/while/body/eval_jaxpr/ppermute | solution.py:15
  341.6 2.6 copy-start
  345.3 9.1 %collective-permute-start.3 = (bf16[256,256]{0,1:T(8,128)(2,1)S(1)}, bf16[256,256]{0,1:T(8,128)(2,1)S(1)}, u32[]{:S(2)}, u32[]{:S(2)}) collective-permute-start(bf16[256,256]{0,1:T(8,128)(2,1)S(1)} %fusion.86), channel_id=1, source_target_pairs={{0,4},{4,8},{8,12},{12,16},{16,20},{20,24},{24,28},{28,0},{1,5},{5... | collective-permute-start | bytes 393224 | tf_op jit(solution)/shard_map/while/body/eval_jaxpr/ppermute | solution.py:15
  346.7 9.2 %collective-permute-start.2 = (bf16[256,256]{0,1:T(8,128)(2,1)S(1)}, bf16[256,256]{0,1:T(8,128)(2,1)S(1)}, u32[]{:S(2)}, u32[]{:S(2)}) collective-permute-start(bf16[256,256]{0,1:T(8,128)(2,1)S(1)} %fusion.85), channel_id=1, source_target_pairs={{0,4},{4,8},{8,12},{12,16},{16,20},{20,24},{24,28},{28,0},{1,5},{5... | collective-permute-start | bytes 393224 | tf_op jit(solution)/shard_map/while/body/eval_jaxpr/ppermute | solution.py:15
  358.3 23.8 %collective-permute-start = (bf16[256,256]{1,0:T(8,128)(2,1)}, bf16[256,256]{1,0:T(8,128)(2,1)}, u32[]{:S(2)}, u32[]{:S(2)}) collective-permute-start(bf16[256,256]{1,0:T(8,128)(2,1)} %copy.227), channel_id=1, source_target_pairs={{0,4},{4,8},{8,12},{12,16},{16,20},{20,24},{24,28},{28,0},{1,5},{5... | collective-permute-start | bytes 393224 | tf_op jit(solution)/shard_map/while/body/eval_jaxpr/ppermute | solution.py:15
  359.8 22.2 %collective-permute-start.1 = (bf16[256,256]{1,0:T(8,128)(2,1)}, bf16[256,256]{1,0:T(8,128)(2,1)}, u32[]{:S(2)}, u32[]{:S(2)}) collective-permute-start(bf16[256,256]{1,0:T(8,128)(2,1)} %copy.228), channel_id=1, source_target_pairs={{0,4},{4,8},{8,12},{12,16},{16,20},{20,24},{24,28},{28,0},{1,5},{5... | collective-permute-start | bytes 393224 | tf_op jit(solution)/shard_map/while/body/eval_jaxpr/ppermute | solution.py:15
  366.6 2.7 copy-start
  370.3 9.1 %collective-permute-start.3 = (bf16[256,256]{0,1:T(8,128)(2,1)S(1)}, bf16[256,256]{0,1:T(8,128)(2,1)S(1)}, u32[]{:S(2)}, u32[]{:S(2)}) collective-permute-start(bf16[256,256]{0,1:T(8,128)(2,1)S(1)} %fusion.86), channel_id=1, source_target_pairs={{0,4},{4,8},{8,12},{12,16},{16,20},{20,24},{24,28},{28,0},{1,5},{5... | collective-permute-start | bytes 393224 | tf_op jit(solution)/shard_map/while/body/eval_jaxpr/ppermute | solution.py:15
  371.4 9.9 %collective-permute-start.2 = (bf16[256,256]{0,1:T(8,128)(2,1)S(1)}, bf16[256,256]{0,1:T(8,128)(2,1)S(1)}, u32[]{:S(2)}, u32[]{:S(2)}) collective-permute-start(bf16[256,256]{0,1:T(8,128)(2,1)S(1)} %fusion.85), channel_id=1, source_target_pairs={{0,4},{4,8},{8,12},{12,16},{16,20},{20,24},{24,28},{28,0},{1,5},{5... | collective-permute-start | bytes 393224 | tf_op jit(solution)/shard_map/while/body/eval_jaxpr/ppermute | solution.py:15
  383.6 22.3 %collective-permute-start = (bf16[256,256]{1,0:T(8,128)(2,1)}, bf16[256,256]{1,0:T(8,128)(2,1)}, u32[]{:S(2)}, u32[]{:S(2)}) collective-permute-start(bf16[256,256]{1,0:T(8,128)(2,1)} %copy.227), channel_id=1, source_target_pairs={{0,4},{4,8},{8,12},{12,16},{16,20},{20,24},{24,28},{28,0},{1,5},{5... | collective-permute-start | bytes 393224 | tf_op jit(solution)/shard_map/while/body/eval_jaxpr/ppermute | solution.py:15
  385.2 20.8 %collective-permute-start.1 = (bf16[256,256]{1,0:T(8,128)(2,1)}, bf16[256,256]{1,0:T(8,128)(2,1)}, u32[]{:S(2)}, u32[]{:S(2)}) collective-permute-start(bf16[256,256]{1,0:T(8,128)(2,1)} %copy.228), channel_id=1, source_target_pairs={{0,4},{4,8},{8,12},{12,16},{16,20},{20,24},{24,28},{28,0},{1,5},{5... | collective-permute-start | bytes 393224 | tf_op jit(solution)/shard_map/while/body/eval_jaxpr/ppermute | solution.py:15
  391.3 2.6 copy-start
  395.1 7.9 %collective-permute-start.3 = (bf16[256,256]{0,1:T(8,128)(2,1)S(1)}, bf16[256,256]{0,1:T(8,128)(2,1)S(1)}, u32[]{:S(2)}, u32[]{:S(2)}) collective-permute-start(bf16[256,256]{0,1:T(8,128)(2,1)S(1)} %fusion.86), channel_id=1, source_target_pairs={{0,4},{4,8},{8,12},{12,16},{16,20},{20,24},{24,28},{28,0},{1,5},{5... | collective-permute-start | bytes 393224 | tf_op jit(solution)/shard_map/while/body/eval_jaxpr/ppermute | solution.py:15
  396.1 9.1 %collective-permute-start.2 = (bf16[256,256]{0,1:T(8,128)(2,1)S(1)}, bf16[256,256]{0,1:T(8,128)(2,1)S(1)}, u32[]{:S(2)}, u32[]{:S(2)}) collective-permute-start(bf16[256,256]{0,1:T(8,128)(2,1)S(1)} %fusion.85), channel_id=1, source_target_pairs={{0,4},{4,8},{8,12},{12,16},{16,20},{20,24},{24,28},{28,0},{1,5},{5... | collective-permute-start | bytes 393224 | tf_op jit(solution)/shard_map/while/body/eval_jaxpr/ppermute | solution.py:15
  407.1 13.0 %all-to-all-start.5 = ((bf16[8,64,256]{2,1,0:T(8,128)(2,1)}), bf16[8,64,256]{2,1,0:T(8,128)(2,1)S(1)}, u32[]{:S(2)}, u32[]{:S(2)}) async-start(bf16[8,64,256]{2,1,0:T(8,128)(2,1)} %copy.132), calls=%async_computation.5 | async-start | bytes 524288 | tf_op jit(solution)/shard_map/all_to_all | solution.py:243
  420.1 16.5 %all-to-all-start.4 = ((bf16[8,64,256]{2,1,0:T(8,128)(2,1)}), bf16[8,64,256]{2,1,0:T(8,128)(2,1)S(1)}, u32[]{:S(2)}, u32[]{:S(2)}) async-start(bf16[8,64,256]{2,1,0:T(8,128)(2,1)} %copy.127), calls=%async_computation.4 | async-start | bytes 524288 | tf_op jit(solution)/shard_map/all_to_all | solution.py:240
  423.6 16.6 %copy-start.7 = (s32[4]{0:T(128)S(1)}, s32[4]{0:T(128)}, u32[]{:S(2)}) copy-start(s32[4]{0:T(128)} %copy-done.6) | copy-start | bytes 52
  436.6 19.9 %all-to-all-start.3 = ((bf16[8,64,1024]{2,1,0:T(8,128)(2,1)}), bf16[8,64,1024]{2,1,0:T(8,128)(2,1)S(1)}, u32[]{:S(2)}, u32[]{:S(2)}) async-start(bf16[8,64,1024]{2,1,0:T(8,128)(2,1)} %copy.122), calls=%async_computation.3 | async-start | bytes 2097152 | tf_op jit(solution)/shard_map/all_to_all | solution.py:237
  440.2 89.0 %reduce-scatter.2.cloned.1.call-start = ((), (), s32[]{:S(2)}) async-start(), calls=%async_computation.9 | async-start | bytes 5242880 | tf_op jit(solution)/shard_map/reduce_scatter | solution.py:262
  476.6 6.1 %copy-start.3 = (bf16[8192,256]{1,0:T(8,128)(2,1)S(1)}, bf16[8192,256]{1,0:T(8,128)(2,1)}, u32[]{:S(2)}) copy-start(bf16[8192,256]{1,0:T(8,128)(2,1)} %param.18) | copy-start | bytes 12582916
  486.0 1.0 copy-start.4
  (1 other events, 1.0 us)
Sparse Core Ops, SparseCore 0:
  9.6 37.1 all-gather.2
  82.7 60.0 all-gather.4
  486.1 42.9 reduce-scatter.1
